TPU v7x, 128 devices: a whole 4x4x4 slice. The times are simulated.
128 devices in a mesh: ep: 32 (over z, x, core), tp: 4 (over y).
Axes of the slice: x: 4, y: 4, z: 4, core: 2. Of those that a mesh axis runs over, the one named last changes fastest.
Arguments:
- weights: bfloat16 [32, 2048, 7168], P('ep', None, 'tp'), may hold values from -6 to 6
- probes: bfloat16 [32, 7168, 256], P('ep', 'tp'), may hold values from -0.0625 to 0.0625
- pairing: int32 [32], replicated, may hold values from 0 to 31, each once
Outputs:
- basis: float32 [32, 2048, 256], P('ep', 'tp')
- factors: bfloat16 [32, 256, 7168], P('ep', None, 'tp')
Inputs may be any that keep to these rules, and one draw needn't show every extreme that they name: `pairing`: entries 2i and 2i+1 name the two experts of pair i; every expert appears exactly once.
All inputs are finite; a program needn't handle non-finite values.
Results may differ from a plain program's by a relative error of at most 0.022.
Values may be sent and summed in bfloat16 or wider, within the bound.
No kernel may reach another device: no remote copies, remote signals or barrier semaphores. Data moves between devices by JAX's collectives and lax.ppermute only.
A program may use at most 64 MiB of HBM per device.

v0:
```python
import math

import jax
import jax.numpy as jnp
from jax import lax
from jax.sharding import PartitionSpec as P

D = 7168
FF = 2048
POWER = 2


def pair_mixer(pairing):
    expert_count = pairing.shape[0]
    expert_ids = jnp.arange(expert_count, dtype=jnp.int32)
    leaders = (pairing[0::2][:, None] == expert_ids[None, :]).astype(jnp.float32)
    followers = (pairing[1::2][:, None] == expert_ids[None, :]).astype(jnp.float32)
    cross = jnp.dot(leaders.T, followers, precision=lax.Precision.HIGHEST)
    return jnp.eye(expert_count, dtype=jnp.float32) + cross + cross.T


def combine_pairs(pair_weights, received):
    return jnp.einsum(
        "ef,fnr->enr", pair_weights, received, precision=lax.Precision.HIGHEST
    ).astype(jnp.bfloat16)


def relay(partial_value, pair_weights):
    rank_cols = partial_value.shape[1]
    ep_count = lax.axis_size("ep")
    tp_count = lax.axis_size("tp")
    device_count = ep_count * tp_count
    received = lax.all_to_all(
        partial_value.reshape(device_count, -1, rank_cols).astype(jnp.bfloat16),
        ("ep", "tp"),
        split_axis=0,
        concat_axis=0,
        tiled=True,
    ).astype(jnp.float32)
    summed = jnp.sum(received.reshape(ep_count, tp_count, -1, rank_cols), axis=1)
    paired = combine_pairs(pair_weights, summed)
    outgoing = jnp.broadcast_to(paired[:, None], (ep_count, tp_count) + paired.shape[1:])
    returned = lax.all_to_all(
        outgoing.reshape(device_count, -1, rank_cols),
        ("ep", "tp"),
        split_axis=0,
        concat_axis=0,
        tiled=True,
    )
    return returned.reshape(-1, rank_cols)


def per_device(weights, probes, pairing):
    weight_block = weights[0]
    probe_block = probes[0]
    pair_weights = pair_mixer(pairing)
    partial_value = jnp.dot(weight_block, probe_block, preferred_element_type=jnp.float32)
    gathered = None
    for sweep in range(POWER + 1):
        if sweep > 0:
            back_proj = jnp.dot(
                weight_block.T, gathered, preferred_element_type=jnp.float32
            ).astype(jnp.bfloat16)
            partial_value = jnp.dot(weight_block, back_proj, preferred_element_type=jnp.float32) / D
        gathered = relay(partial_value, pair_weights)
    gram_matrix = jnp.dot(gathered.T, gathered, preferred_element_type=jnp.float32)
    lower_factor = jnp.linalg.cholesky(gram_matrix)
    basis_cols = jax.scipy.linalg.solve_triangular(
        lower_factor, gathered.astype(jnp.float32).T, lower=True
    ).T
    row_count = weight_block.shape[0] // lax.axis_size("tp")
    own_rows = lax.dynamic_slice_in_dim(basis_cols, lax.axis_index("tp") * row_count, row_count, 0)
    basis = (own_rows * math.sqrt(FF))[None]
    factors = jnp.dot(
        basis_cols.astype(jnp.bfloat16).T, weight_block, preferred_element_type=jnp.float32
    ).astype(jnp.bfloat16)[None]
    return (basis, factors)


def solution(mesh):
    placed = (P("ep", None, "tp"), P("ep", "tp", None), P())
    return jax.shard_map(
        per_device,
        mesh=mesh,
        in_specs=placed,
        out_specs=(P("ep", "tp", None), P("ep", None, "tp")),
        check_vma=False,
    )
```

profile of v0, /device:TPU:1, one launch (start us, length us, event | category | flops | bytes accessed | tf_op | source)
XLA Modules:
  0.0 251.8 jit_solution(14354439393962782600)
XLA Ops:
  0.6 1.2 copy-done
  1.8 6.2 %convolution_convert_fusion = bf16[128,16,256]{2,1,0:T(8,128)(2,1)} fusion(bf16[128,16,1792]{2,1,0:T(8,128)(2,1)} %bitcast.135, bf16[1,1792,256]{2,1,0:T(8,128)(2,1)S(1)} %copy-done), kind=kOutput, calls=%fused_computation.30 | convolution fusion | flops 1879572480 | bytes 9306112 | tf_op jit(solution)/shard_map/dot_general | solution.py:57
  8.0 11.5 %all-to-all-start = ((bf16[128,16,256]{2,1,0:T(8,128)(2,1)}), bf16[128,16,256]{2,1,0:T(8,128)(2,1)S(1)}, u32[]{:S(2)}, u32[]{:S(2)}) async-start(bf16[128,16,256]{2,1,0:T(8,128)(2,1)} %convolution_convert_fusion), calls=%async_computation | async-start | bytes 2097152 | tf_op jit(solution)/shard_map/all_to_all | solution.py:33
  20.0 18.9 %all-to-all-done = bf16[128,16,256]{2,1,0:T(8,128)(2,1)S(1)} async-done(((bf16[128,16,256]{2,1,0:T(8,128)(2,1)}), bf16[128,16,256]{2,1,0:T(8,128)(2,1)S(1)}, u32[]{:S(2)}, u32[]{:S(2)}) %all-to-all-start) | async-done | bytes 1048608 | tf_op jit(solution)/shard_map/all_to_all | solution.py:33
  40.2 23.0 %all_to_all.30 = bf16[128,16,256]{2,1,0:T(8,128)(2,1)S(1)} all-to-all(bf16[128,16,256]{2,1,0:T(8,128)(2,1)S(1)} %bitcast.127), channel_id=1, replica_groups=mesh['ep'=32,'tp'=4] {'ep','tp'}, dimensions={0} | all-to-all | bytes 2097152 | tf_op jit(solution)/shard_map/all_to_all | solution.py:43
  63.2 10.1 %fusion.31 = bf16[2048,256]{0,1:T(8,128)(2,1)S(1)} fusion(bf16[1,2048,1792]{2,1,0:T(8,128)(2,1)} %param.3, bf16[2048,256]{1,0:T(8,128)(2,1)S(1)} %bitcast.133), kind=kOutput, calls=%fused_computation.22 | convolution fusion | flops 3759603712 | bytes 9437184 | tf_op jit(solution)/shard_map/dot_general | solution.py:64
  73.9 23.0 %all_to_all.31 = bf16[128,16,256]{2,1,0:T(8,128)(2,1)S(1)} all-to-all(bf16[128,16,256]{2,1,0:T(8,128)(2,1)S(1)} %bitcast.131), channel_id=1, replica_groups=mesh['ep'=32,'tp'=4] {'ep','tp'}, dimensions={0} | all-to-all | bytes 2097152 | tf_op jit(solution)/shard_map/all_to_all | solution.py:33
  98.2 23.0 %all_to_all.32 = bf16[128,16,256]{2,1,0:T(8,128)(2,1)S(1)} all-to-all(bf16[128,16,256]{2,1,0:T(8,128)(2,1)S(1)} %bitcast.128), channel_id=1, replica_groups=mesh['ep'=32,'tp'=4] {'ep','tp'}, dimensions={0} | all-to-all | bytes 2097152 | tf_op jit(solution)/shard_map/all_to_all | solution.py:43
  121.2 10.1 %fusion.34 = bf16[2048,256]{0,1:T(8,128)(2,1)S(1)} fusion(bf16[1,2048,1792]{2,1,0:T(8,128)(2,1)} %param.3, bf16[2048,256]{1,0:T(8,128)(2,1)S(1)} %bitcast.134), kind=kOutput, calls=%fused_computation.23 | convolution fusion | flops 3759603712 | bytes 9437184 | tf_op jit(solution)/shard_map/dot_general | solution.py:64
  131.9 23.0 %all_to_all.33 = bf16[128,16,256]{2,1,0:T(8,128)(2,1)S(1)} all-to-all(bf16[128,16,256]{2,1,0:T(8,128)(2,1)S(1)} %bitcast.132), channel_id=1, replica_groups=mesh['ep'=32,'tp'=4] {'ep','tp'}, dimensions={0} | all-to-all | bytes 2097152 | tf_op jit(solution)/shard_map/all_to_all | solution.py:33
  156.1 1.1 broadcast_in_dim.13
  157.2 3.8 %all-to-all-start.5 = ((bf16[128,16,256]{2,1,0:T(8,128)(2,1)}), bf16[128,16,256]{2,1,0:T(8,128)(2,1)S(1)}, u32[]{:S(2)}, u32[]{:S(2)}) async-start(bf16[128,16,256]{2,1,0:T(8,128)(2,1)} %bitcast.19), calls=%async_computation.5 | async-start | bytes 2097152 | tf_op jit(solution)/shard_map/all_to_all | solution.py:43
  161.0 19.5 %all-to-all-done.5 = bf16[128,16,256]{2,1,0:T(8,128)(2,1)S(1)} async-done(((bf16[128,16,256]{2,1,0:T(8,128)(2,1)}), bf16[128,16,256]{2,1,0:T(8,128)(2,1)S(1)}, u32[]{:S(2)}, u32[]{:S(2)}) %all-to-all-start.5) | async-done | bytes 1048608 | tf_op jit(solution)/shard_map/all_to_all | solution.py:43
  181.2 11.7 %cholesky.50 = f32[128,128]{1,0:T(8,128)S(1)} custom-call(f32[128,128]{1,0:T(8,128)S(1)} %cholesky.118), custom_call_target="Cholesky" | custom-call | tf_op jit(solution)/shard_map/jit(cholesky)/cholesky | solution.py:67
  193.0 9.8 %custom-call.15 = f32[1,128,128]{1,2,0:T(8,128)S(1)} custom-call(f32[1,128,128]{2,1,0:T(8,128)S(1)} %get-tuple-element.31), custom_call_target="InvertDiagBlocksLowerTriangular" | custom-call | tf_op jit(solution)/shard_map/jit(cholesky)/cholesky | solution.py:67
  203.3 11.7 %cholesky.105 = f32[128,128]{1,0:T(8,128)S(1)} custom-call(f32[128,128]{1,0:T(8,128)S(1)} %convolution_subtract_fusion.1), custom_call_target="Cholesky" | custom-call | tf_op jit(solution)/shard_map/jit(cholesky)/cholesky | solution.py:67
  217.2 4.1 %while.1 = (s32[]{:T(128)}, f32[256,256]{1,0:T(8,128)S(1)}, s32[2,2]{1,0:T(2,128)S(1)}, f32[2,128,128]{2,1,0:T(8,128)S(1)}, s32[]{:T(128)}) while((s32[]{:T(128)}, f32[256,256]{1,0:T(8,128)S(1)}, s32[2,2]{1,0:T(2,128)S(1)}, f32[2,128,128]{2,1,0:T(8,128)S(1)}, s32[]{:T(128)}) %tuple.31), condition=%wide.while_cond, body=%wide.while_body.sunk | while | flops 2 | bytes 131189 | solution.py:68
  217.8 1.4 bitcast_dynamic-update-slice_fusion.2
  219.9 1.4 bitcast_dynamic-update-slice_fusion.2
  221.3 19.9 %custom-call.16 = f32[2,128,128]{1,2,0:T(8,128)S(1)} custom-call(f32[2,128,128]{2,1,0:T(8,128)S(1)} %get-tuple-element.9), custom_call_target="InvertDiagBlocksLowerTriangular" | custom-call | tf_op jit(solution)/shard_map/jit(_solve_triangular)/triangular_solve | solution.py:68
  242.6 1.0 convolution_subtract_fusion
  243.6 1.1 fusion.57
  244.6 6.1 %fusion.37 = bf16[1,256,1792]{2,1,0:T(8,128)(2,1)} fusion(bf16[1,2048,1792]{2,1,0:T(8,128)(2,1)} %param.3, f32[128,2048]{1,0:T(8,128)S(1)} %fusion.57, f32[128,2048]{1,0:T(8,128)S(1)} %fusion.50), kind=kOutput, calls=%fused_computation.24 | convolution fusion | flops 1881604096 | bytes 10354688 | tf_op jit(solution)/shard_map/dot_general | solution.py:74
  250.8 1.0 copy.58
  (41 shorter events, 9.9 us)
Async XLA Ops:
  0.6 1.2 copy-start
  1.8 17.7 %copy-start.1 = (s32[32]{0:T(128)S(1)}, s32[32]{0:T(128)}, u32[]{:S(2)}) copy-start(s32[32]{0:T(128)} %param.5) | copy-start | bytes 388
  8.0 30.9 %all-to-all-start = ((bf16[128,16,256]{2,1,0:T(8,128)(2,1)}), bf16[128,16,256]{2,1,0:T(8,128)(2,1)S(1)}, u32[]{:S(2)}, u32[]{:S(2)}) async-start(bf16[128,16,256]{2,1,0:T(8,128)(2,1)} %convolution_convert_fusion), calls=%async_computation | async-start | bytes 2097152 | tf_op jit(solution)/shard_map/all_to_all | solution.py:33
  157.2 23.4 %all-to-all-start.5 = ((bf16[128,16,256]{2,1,0:T(8,128)(2,1)}), bf16[128,16,256]{2,1,0:T(8,128)(2,1)S(1)}, u32[]{:S(2)}, u32[]{:S(2)}) async-start(bf16[128,16,256]{2,1,0:T(8,128)(2,1)} %bitcast.19), calls=%async_computation.5 | async-start | bytes 2097152 | tf_op jit(solution)/shard_map/all_to_all | solution.py:43
where the time goes:
time: 252 us
  blocking collectives  92.2 us (37%)
  other arithmetic  54.6 us (22%)
  matrix products  38.9 us (15%)
  waiting for transfers between devices  38.4 us (15%)
  starting transfers between devices  15.3 us (6%)
  local copies, waits for them, and re-layouts  10.1 us (4%)
    all_to_all x2, blocking collectives, relay(): lax.all_to_all(outgoing.reshape(device_count, -1, rank_cols), ('ep', 'tp'...  46.1 us
    all_to_all x2, blocking collectives, relay(): lax.all_to_all(partial_value.reshape(device_count, -1, rank_cols).astype(...  46.1 us
    another operation x6, other arithmetic, per_device(): lower_factor = jnp.linalg.cholesky(gram_matrix)  34 us
    dot_general x2, matrix products, per_device(): jnp.dot(weight_block, back_proj, preferred_element_type=jnp.float32) / D  20.2 us
    another operation x3, other arithmetic, per_device(): jax.scipy.linalg.solve_triangular(lower_factor, gathered.astype(jnp.float...  20 us
    all_to_all x1, waiting for transfers between devices, relay(): lax.all_to_all(outgoing.reshape(device_count, -1, rank_cols), ('ep', 'tp'...  19.5 us
    all_to_all x1, waiting for transfers between devices, relay(): lax.all_to_all(partial_value.reshape(device_count, -1, rank_cols).astype(...  18.9 us
    all_to_all x1, starting transfers between devices, relay(): lax.all_to_all(partial_value.reshape(device_count, -1, rank_cols).astype(...  11.5 us
  transfers between devices with their start and end apart: 2, of which 2 were waited for; matrix products, arithmetic and copies ran while one was open for 0% of the time, Pallas kernels for 0%

commit v1 on v0

v1 whole, which is shorter than its diff:
```python
import math

import jax
import jax.numpy as jnp
from jax import lax
from jax.experimental import pallas as pl
from jax.experimental.pallas import tpu as pltpu
from jax.sharding import PartitionSpec as P

D = 7168
FF = 2048
POWER = 2
F32 = jnp.float32
BF16 = jnp.bfloat16
HIGHEST = lax.Precision.HIGHEST
BLOCK = 64
TILE = 256
VMEM_LIMIT = 40 * 1024 * 1024


def params():
    return pltpu.CompilerParams(vmem_limit_bytes=VMEM_LIMIT)


def vmem_spec():
    return pl.BlockSpec(memory_space=pltpu.VMEM)


def any_spec():
    return pl.BlockSpec(memory_space=pl.ANY)


def smem_spec():
    return pl.BlockSpec(memory_space=pltpu.SMEM)


def mm(a, b):
    return jnp.dot(a, b, preferred_element_type=F32)


def row_copies(weights, held, sems):
    rows = held.shape[0]
    return [
        pltpu.make_async_copy(
            weights.at[pl.ds(s, TILE), :], held.at[pl.ds(s, TILE), :], sems.at[n]
        )
        for n, s in enumerate(range(0, rows, TILE))
    ]


def column_copies(weights, held, sems):
    columns = held.shape[1]
    return [
        pltpu.make_async_copy(
            weights.at[:, pl.ds(s, TILE)], held.at[:, pl.ds(s, TILE)], sems.at[n]
        )
        for n, s in enumerate(range(0, columns, TILE))
    ]


def first_kernel(weights, probes, out, held, sems):
    copies = row_copies(weights, held, sems)
    for copy in copies:
        copy.start()
    for n, copy in enumerate(copies):
        copy.wait()
        s = n * TILE
        out[s : s + TILE, :] = mm(held[s : s + TILE, :], probes[...]).astype(BF16)


def power_kernel(weights, sketch, out, held, turned, back, sems):
    copies = column_copies(weights, held, sems)
    for copy in copies:
        copy.start()
    turned[...] = sketch[...].T
    for n, copy in enumerate(copies):
        copy.wait()
        s = n * TILE
        back[s : s + TILE, :] = mm(turned[...], held[:, s : s + TILE]).astype(BF16).T
    for s in range(0, out.shape[0], TILE):
        out[s : s + TILE, :] = (mm(held[s : s + TILE, :], back[...]) * (1.0 / D)).astype(BF16)


def pair_kernel(pairing, received, out):
    tp_count = out.shape[0] // pairing.shape[0]

    def total(expert):
        rows = received[pl.ds(expert * tp_count, tp_count)].astype(F32)
        return jnp.sum(rows, axis=0)

    for i in range(pairing.shape[0] // 2):
        a = pairing[2 * i]
        b = pairing[2 * i + 1]
        both = (total(a) + total(b)).astype(BF16)
        spread = jnp.broadcast_to(both[None], (tp_count,) + both.shape)
        out[pl.ds(a * tp_count, tp_count)] = spread
        out[pl.ds(b * tp_count, tp_count)] = spread


def factor_block(work):
    sublane = lax.broadcasted_iota(jnp.int32, (8, 2 * BLOCK), 0)

    def row(x, i):
        return jnp.broadcast_to(x[i : i + 1, :], x.shape)

    def column(x, c):
        return jnp.broadcast_to(x[:, c : c + 1], x.shape)

    count = BLOCK // 8
    groups = [work[8 * g : 8 * g + 8, :] for g in range(count)]
    for p in range(count):
        columns = {
            g: [column(groups[g], 8 * p + i) for i in range(8)] for g in range(p, count)
        }
        pivots = jnp.ones_like(groups[p])
        for i in range(8):
            pivot = row(columns[p][i], i)
            pivots = jnp.where(sublane == i, pivot, pivots)
            inverse = 1.0 / pivot
            across = [row(columns[p][c], i) for c in range(i + 1, 8)]
            pivot_row = row(groups[p], i)
            for g in range(p, count):
                if g == p and i == 7:
                    continue
                scaled = columns[g][i] * inverse
                if g == p:
                    scaled = jnp.where(sublane > i, scaled, 0.0)
                for n, c in enumerate(range(i + 1, 8)):
                    columns[g][c] = columns[g][c] - scaled * across[n]
                groups[g] = groups[g] - scaled * pivot_row
        work[8 * p : 8 * p + 8, :] = groups[p] * lax.rsqrt(pivots)


def inverse_factor(gram, inverse, work):
    size = gram.shape[0]

    def identity(n):
        rows = lax.broadcasted_iota(jnp.int32, (n, n), 0)
        columns = lax.broadcasted_iota(jnp.int32, (n, n), 1)
        return jnp.where(rows == columns, 1.0, 0.0).astype(F32)

    inverse[...] = identity(size)
    for s in range(0, size, BLOCK):
        e = s + BLOCK
        work[:, 0:BLOCK] = gram[s:e, s:e]
        work[:, BLOCK : 2 * BLOCK] = identity(BLOCK)
        factor_block(work)
        block = work[:, BLOCK : 2 * BLOCK]
        done = jnp.dot(block, inverse[s:e, :], precision=HIGHEST, preferred_element_type=F32)
        inverse[s:e, :] = done
        if e < size:
            upper = jnp.dot(block, gram[s:e, :], precision=HIGHEST, preferred_element_type=F32)
            left = upper[:, e:]
            turned = (((0,), (0,)), ((), ()))
            gram[e:, :] = gram[e:, :] - lax.dot_general(
                left, upper, turned, precision=HIGHEST, preferred_element_type=F32
            )
            inverse[e:, :] = inverse[e:, :] - lax.dot_general(
                left, done, turned, precision=HIGHEST, preferred_element_type=F32
            )


def final_kernel(
    start, weights, sketch, basis, factors, held, turned, mixed, gram, inverse, work, sems
):
    copies = column_copies(weights, held, sems)
    for copy in copies:
        copy.start()
    turned[...] = sketch[...].T
    gram[...] = mm(turned[...], sketch[...])
    inverse_factor(gram, inverse, work)
    high = inverse[...].astype(BF16)
    low = (inverse[...] - high.astype(F32)).astype(BF16)
    for s in range(0, sketch.shape[0], TILE):
        part = turned[:, s : s + TILE]
        mixed[:, s : s + TILE] = (mm(high, part) + mm(low, part)).astype(BF16)
    own_count = basis.shape[0]
    own = sketch[pl.ds(pl.multiple_of(start[0] * own_count, own_count), own_count), :]
    basis[...] = (mm(own, high.T) + mm(own, low.T)) * math.sqrt(FF)
    for n, copy in enumerate(copies):
        copy.wait()
        s = n * TILE
        factors[:, s : s + TILE] = mm(mixed[...], held[:, s : s + TILE]).astype(BF16)


def exchange(value):
    return lax.all_to_all(value, ("ep", "tp"), split_axis=0, concat_axis=0, tiled=True)


def per_device(weights, probes, pairing):
    weight_block = weights[0]
    probe_block = probes[0]
    rows, columns = weight_block.shape
    rank = probe_block.shape[1]
    device_count = lax.axis_size("ep") * lax.axis_size("tp")
    own_count = rows // lax.axis_size("tp")
    held = pltpu.VMEM((rows, columns), BF16)
    row_sems = pltpu.SemaphoreType.DMA((rows // TILE,))
    column_sems = pltpu.SemaphoreType.DMA((columns // TILE,))
    sketch_shape = jax.ShapeDtypeStruct((rows, rank), BF16)
    chunks = (device_count, rows // device_count, rank)

    def relay(partial_value):
        received = exchange(partial_value.reshape(chunks))
        paired = pl.pallas_call(
            pair_kernel,
            out_shape=jax.ShapeDtypeStruct(chunks, BF16),
            in_specs=[smem_spec(), vmem_spec()],
            out_specs=vmem_spec(),
            name="pair",
        )(pairing, received)
        return exchange(paired).reshape(rows, rank)

    partial_value = pl.pallas_call(
        first_kernel,
        out_shape=sketch_shape,
        in_specs=[any_spec(), vmem_spec()],
        out_specs=vmem_spec(),
        scratch_shapes=[held, row_sems],
        compiler_params=params(),
        name="first",
    )(weight_block, probe_block)
    sketch = relay(partial_value)
    for _ in range(POWER):
        partial_value = pl.pallas_call(
            power_kernel,
            out_shape=sketch_shape,
            in_specs=[any_spec(), vmem_spec()],
            out_specs=vmem_spec(),
            scratch_shapes=[
                held,
                pltpu.VMEM((rank, rows), BF16),
                pltpu.VMEM((columns, rank), BF16),
                column_sems,
            ],
            compiler_params=params(),
            name="power",
        )(weight_block, sketch)
        sketch = relay(partial_value)
    start = lax.axis_index("tp").reshape(1).astype(jnp.int32)
    basis, factors = pl.pallas_call(
        final_kernel,
        out_shape=(
            jax.ShapeDtypeStruct((own_count, rank), F32),
            jax.ShapeDtypeStruct((rank, columns), BF16),
        ),
        in_specs=[smem_spec(), any_spec(), vmem_spec()],
        out_specs=(vmem_spec(), vmem_spec()),
        scratch_shapes=[
            held,
            pltpu.VMEM((rank, rows), BF16),
            pltpu.VMEM((rank, rows), BF16),
            pltpu.VMEM((rank, rank), F32),
            pltpu.VMEM((rank, rank), F32),
            pltpu.VMEM((BLOCK, 2 * BLOCK), F32),
            column_sems,
        ],
        compiler_params=params(),
        name="final",
    )(start, weight_block, sketch)
    return (basis[None], factors[None])


def solution(mesh):
    placed = (P("ep", None, "tp"), P("ep", "tp", None), P())
    return jax.shard_map(
        per_device,
        mesh=mesh,
        in_specs=placed,
        out_specs=(P("ep", "tp", None), P("ep", None, "tp")),
        check_vma=False,
    )
```

time: 252 us -> 211 us (0.84)
  other arithmetic: 54.6 us -> 0 us
  Pallas kernels: 0 us -> 47.6 us
  matrix products: 38.9 us -> 0 us
  blocking collectives: 92.2 us -> 125 us
  waiting for transfers between devices: 38.4 us -> 19.5 us
  starting transfers between devices: 15.3 us -> 3.83 us
  local copies, waits for them, and re-layouts: 10.1 us -> 13.5 us
    another operation x9 -> x0, other arithmetic: 54 us -> none  [the longest x6 34 us: per_device(): lower_factor = jnp.linalg.cholesky(gram_matrix)]
    pallas_call x0 -> x7, Pallas kernels: none -> 47.6 us  [the longest x1 17.7 us: per_device(): pl.pallas_call(final_kernel, out_shape=(jax.ShapeDtypeStruct((own_count,...]
    dot_general x9 -> x0, matrix products: 35.7 us -> none  [the longest x2 20.2 us: per_device(): jnp.dot(weight_block, back_proj, preferred_element_type=jnp.float32) / D]
    all_to_all x4 -> x5, blocking collectives: 92.2 us -> 125 us  [exchange(): lax.all_to_all(value, ('ep', 'tp'), split_axis=0, concat_axis=0, tiled=True)]
    all_to_all x2 -> x1, waiting for transfers between devices: 38.4 us -> 19.5 us  [exchange(): lax.all_to_all(value, ('ep', 'tp'), split_axis=0, concat_axis=0, tiled=True)]
    all_to_all x2 -> x1, starting transfers between devices: 15.3 us -> 3.83 us  [exchange(): lax.all_to_all(value, ('ep', 'tp'), split_axis=0, concat_axis=0, tiled=True)]
    unnamed x5 -> x10, local copies, waits for them, and re-layouts: 2.18 us -> 13.5 us
    another operation x9 -> x0, local copies, waits for them, and re-layouts: 4.16 us -> none
  transfers between devices with their start and end apart: 2 -> 1, of which waited for: 2 -> 1; matrix products, arithmetic and copies ran while one was open for 0% -> 0% of each run, Pallas kernels for 0% -> 0%
where the time goes in v1:
time: 211 us; the launch traced here: 210 us
  blocking collectives  125 us (59%)
  Pallas kernels  47.6 us (23%)
  waiting for transfers between devices  19.5 us (9%)
  local copies, waits for them, and re-layouts  13.5 us (6%)
  starting transfers between devices  3.83 us (2%)
    all_to_all x5, blocking collectives, exchange(): lax.all_to_all(value, ('ep', 'tp'), split_axis=0, concat_axis=0, tiled=True)  125 us
    all_to_all x1, waiting for transfers between devices, exchange(): lax.all_to_all(value, ('ep', 'tp'), split_axis=0, concat_axis=0, tiled=True)  19.5 us
    pallas_call x1, Pallas kernels, per_device(): pl.pallas_call(final_kernel, out_shape=(jax.ShapeDtypeStruct((own_count,...  17.7 us
    pallas_call x2, Pallas kernels, per_device(): pl.pallas_call(power_kernel, out_shape=sketch_shape, in_specs=[any_spec()...  16 us
    unnamed x10, local copies, waits for them, and re-layouts  13.5 us
    pallas_call x3, Pallas kernels, relay(): pl.pallas_call(pair_kernel, out_shape=jax.ShapeDtypeStruct(chunks, BF16),...  7.15 us
    pallas_call x1, Pallas kernels, per_device(): pl.pallas_call(first_kernel, out_shape=sketch_shape, in_specs=[any_spec()...  6.82 us
  transfers between devices with their start and end apart: 1, of which 1 were waited for; matrix products, arithmetic and copies ran while one was open for 0% of the time, Pallas kernels for 0%

profile of v1, /device:TPU:1, one launch (start us, length us, event | category | flops | bytes accessed | tf_op | source)
XLA Modules:
  0.0 210.3 jit_solution(14467106278389598751)
XLA Ops:
  0.6 0.0 copy-start
  0.6 3.1 %copy-done = bf16[1,2048,1792]{2,1,0:T(8,128)(2,1)S(1)} copy-done((bf16[1,2048,1792]{2,1,0:T(8,128)(2,1)S(1)}, bf16[1,2048,1792]{2,1,0:T(8,128)(2,1)}, u32[]{:S(2)}) %copy-start) | copy-done | bytes 7340056
  3.7 0.0 copy-start.4
  3.7 1.2 copy-done.4
  4.9 6.8 %first.1 = bf16[2048,256]{1,0:T(8,128)(2,1)S(1)} custom-call(bf16[2048,1792]{1,0:T(8,128)(2,1)S(1)} %bitcast.11, bf16[1792,256]{1,0:T(8,128)(2,1)S(1)} %bitcast.21), custom_call_target="tpu_custom_call" | custom-call | tf_op jit(solution)/shard_map/first/pallas_call | solution.py:214
  11.7 30.8 %all_to_all.30.received = bf16[128,16,256]{2,1,0:T(8,128)(2,1)} all-to-all(bf16[128,16,256]{2,1,0:T(8,128)(2,1)S(1)} %bitcast.20), channel_id=1, replica_groups=mesh['ep'=32,'tp'=4] {'ep','tp'}, dimensions={0} | all-to-all | bytes 2097152 | tf_op jit(solution)/shard_map/all_to_all | solution.py:187
  42.6 2.4 %pair.3 = bf16[128,16,256]{2,1,0:T(8,128)(2,1)} custom-call(s32[32]{0:T(128)} %pairing.5, bf16[128,16,256]{2,1,0:T(8,128)(2,1)} %all_to_all.30.received), custom_call_target="tpu_custom_call" | custom-call | tf_op jit(solution)/shard_map/pair/pallas_call | solution.py:205
  45.0 23.6 %all_to_all.31 = bf16[128,16,256]{2,1,0:T(8,128)(2,1)S(1)} all-to-all(bf16[128,16,256]{2,1,0:T(8,128)(2,1)} %pair.3), channel_id=1, replica_groups=mesh['ep'=32,'tp'=4] {'ep','tp'}, dimensions={0} | all-to-all | bytes 2097152 | tf_op jit(solution)/shard_map/all_to_all | solution.py:187
  68.6 0.0 copy-start.1
  68.6 3.1 %copy-done.1 = bf16[1,2048,1792]{2,1,0:T(8,128)(2,1)S(1)} copy-done((bf16[1,2048,1792]{2,1,0:T(8,128)(2,1)S(1)}, bf16[1,2048,1792]{2,1,0:T(8,128)(2,1)}, u32[]{:S(2)}) %copy-start.1) | copy-done | bytes 7340056
  71.7 8.0 %power.2 = bf16[2048,256]{1,0:T(8,128)(2,1)S(1)} custom-call(bf16[2048,1792]{1,0:T(8,128)(2,1)S(1)} %bitcast.12, bf16[2048,256]{1,0:T(8,128)(2,1)S(1)} %bitcast.16), custom_call_target="tpu_custom_call" | custom-call | tf_op jit(solution)/shard_map/power/pallas_call | solution.py:225
  79.6 23.4 %all_to_all.32.received = bf16[128,16,256]{2,1,0:T(8,128)(2,1)} all-to-all(bf16[128,16,256]{2,1,0:T(8,128)(2,1)S(1)} %bitcast.17), channel_id=1, replica_groups=mesh['ep'=32,'tp'=4] {'ep','tp'}, dimensions={0} | all-to-all | bytes 2097152 | tf_op jit(solution)/shard_map/all_to_all | solution.py:187
  103.1 2.4 %pair.4 = bf16[128,16,256]{2,1,0:T(8,128)(2,1)} custom-call(s32[32]{0:T(128)} %pairing.5, bf16[128,16,256]{2,1,0:T(8,128)(2,1)} %all_to_all.32.received), custom_call_target="tpu_custom_call" | custom-call | tf_op jit(solution)/shard_map/pair/pallas_call | solution.py:205
  105.5 23.6 %all_to_all.33 = bf16[128,16,256]{2,1,0:T(8,128)(2,1)S(1)} all-to-all(bf16[128,16,256]{2,1,0:T(8,128)(2,1)} %pair.4), channel_id=1, replica_groups=mesh['ep'=32,'tp'=4] {'ep','tp'}, dimensions={0} | all-to-all | bytes 2097152 | tf_op jit(solution)/shard_map/all_to_all | solution.py:187
  129.1 0.0 copy-start.2
  129.1 3.1 %copy-done.2 = bf16[1,2048,1792]{2,1,0:T(8,128)(2,1)S(1)} copy-done((bf16[1,2048,1792]{2,1,0:T(8,128)(2,1)S(1)}, bf16[1,2048,1792]{2,1,0:T(8,128)(2,1)}, u32[]{:S(2)}) %copy-start.2) | copy-done | bytes 7340056
  132.2 8.0 %power.3 = bf16[2048,256]{1,0:T(8,128)(2,1)S(1)} custom-call(bf16[2048,1792]{1,0:T(8,128)(2,1)S(1)} %bitcast.13, bf16[2048,256]{1,0:T(8,128)(2,1)S(1)} %bitcast.18), custom_call_target="tpu_custom_call" | custom-call | tf_op jit(solution)/shard_map/power/pallas_call | solution.py:225
  140.2 23.4 %all_to_all.34.received = bf16[128,16,256]{2,1,0:T(8,128)(2,1)} all-to-all(bf16[128,16,256]{2,1,0:T(8,128)(2,1)S(1)} %bitcast.19), channel_id=1, replica_groups=mesh['ep'=32,'tp'=4] {'ep','tp'}, dimensions={0} | all-to-all | bytes 2097152 | tf_op jit(solution)/shard_map/all_to_all | solution.py:187
  163.6 2.3 %pair.5 = bf16[128,16,256]{2,1,0:T(8,128)(2,1)} custom-call(s32[32]{0:T(128)} %pairing.5, bf16[128,16,256]{2,1,0:T(8,128)(2,1)} %all_to_all.34.received), custom_call_target="tpu_custom_call" | custom-call | tf_op jit(solution)/shard_map/pair/pallas_call | solution.py:205
  165.9 3.8 %all-to-all-start.5 = ((bf16[128,16,256]{2,1,0:T(8,128)(2,1)}), bf16[128,16,256]{2,1,0:T(8,128)(2,1)S(1)}, u32[]{:S(2)}, u32[]{:S(2)}) async-start(bf16[128,16,256]{2,1,0:T(8,128)(2,1)} %pair.5), calls=%async_computation.5 | async-start | bytes 2097152 | tf_op jit(solution)/shard_map/all_to_all | solution.py:187
  169.8 19.5 %all-to-all-done.5 = bf16[128,16,256]{2,1,0:T(8,128)(2,1)S(1)} async-done(((bf16[128,16,256]{2,1,0:T(8,128)(2,1)}), bf16[128,16,256]{2,1,0:T(8,128)(2,1)S(1)}, u32[]{:S(2)}, u32[]{:S(2)}) %all-to-all-start.5) | async-done | bytes 1048608 | tf_op jit(solution)/shard_map/all_to_all | solution.py:187
  189.3 0.0 copy-start.3
  189.3 3.1 %copy-done.3 = bf16[1,2048,1792]{2,1,0:T(8,128)(2,1)S(1)} copy-done((bf16[1,2048,1792]{2,1,0:T(8,128)(2,1)S(1)}, bf16[1,2048,1792]{2,1,0:T(8,128)(2,1)}, u32[]{:S(2)}) %copy-start.3) | copy-done | bytes 7340056
  192.4 17.7 %final.1 = (f32[512,256]{1,0:T(8,128)}, bf16[256,1792]{1,0:T(8,128)(2,1)}) custom-call(s32[1]{0:T(128)} %bitcast.start, bf16[2048,1792]{1,0:T(8,128)(2,1)S(1)} %bitcast.14, bf16[2048,256]{1,0:T(8,128)(2,1)S(1)} %bitcast.15), custom_call_target="tpu_custom_call" | custom-call | tf_op jit(solution)/shard_map/final/pallas_call | solution.py:241
Async XLA Ops:
  0.6 3.1 %copy-start = (bf16[1,2048,1792]{2,1,0:T(8,128)(2,1)S(1)}, bf16[1,2048,1792]{2,1,0:T(8,128)(2,1)}, u32[]{:S(2)}) copy-start(bf16[1,2048,1792]{2,1,0:T(8,128)(2,1)} %param.3) | copy-start | bytes 22020100
  3.7 1.2 copy-start.4
  68.6 3.1 %copy-start.1 = (bf16[1,2048,1792]{2,1,0:T(8,128)(2,1)S(1)}, bf16[1,2048,1792]{2,1,0:T(8,128)(2,1)}, u32[]{:S(2)}) copy-start(bf16[1,2048,1792]{2,1,0:T(8,128)(2,1)} %param.3) | copy-start | bytes 22020100
  129.1 3.1 %copy-start.2 = (bf16[1,2048,1792]{2,1,0:T(8,128)(2,1)S(1)}, bf16[1,2048,1792]{2,1,0:T(8,128)(2,1)}, u32[]{:S(2)}) copy-start(bf16[1,2048,1792]{2,1,0:T(8,128)(2,1)} %param.3) | copy-start | bytes 22020100
  165.9 23.4 %all-to-all-start.5 = ((bf16[128,16,256]{2,1,0:T(8,128)(2,1)}), bf16[128,16,256]{2,1,0:T(8,128)(2,1)S(1)}, u32[]{:S(2)}, u32[]{:S(2)}) async-start(bf16[128,16,256]{2,1,0:T(8,128)(2,1)} %pair.5), calls=%async_computation.5 | async-start | bytes 2097152 | tf_op jit(solution)/shard_map/all_to_all | solution.py:187
  189.3 3.1 %copy-start.3 = (bf16[1,2048,1792]{2,1,0:T(8,128)(2,1)S(1)}, bf16[1,2048,1792]{2,1,0:T(8,128)(2,1)}, u32[]{:S(2)}) copy-start(bf16[1,2048,1792]{2,1,0:T(8,128)(2,1)} %param.3) | copy-start | bytes 22020100

commit v2 on v1

--- a/solution.py
+++ b/solution.py
@@ -15,7 +15,7 @@
 HIGHEST = lax.Precision.HIGHEST
 BLOCK = 64
 TILE = 256
-VMEM_LIMIT = 40 * 1024 * 1024
+VMEM_LIMIT = 24 * 1024 * 1024
 
 
 def params():
@@ -26,10 +26,6 @@
     return pl.BlockSpec(memory_space=pltpu.VMEM)
 
 
-def any_spec():
-    return pl.BlockSpec(memory_space=pl.ANY)
-
-
 def smem_spec():
     return pl.BlockSpec(memory_space=pltpu.SMEM)
 
@@ -38,47 +34,18 @@
     return jnp.dot(a, b, preferred_element_type=F32)
 
 
-def row_copies(weights, held, sems):
-    rows = held.shape[0]
-    return [
-        pltpu.make_async_copy(
-            weights.at[pl.ds(s, TILE), :], held.at[pl.ds(s, TILE), :], sems.at[n]
-        )
-        for n, s in enumerate(range(0, rows, TILE))
-    ]
-
-
-def column_copies(weights, held, sems):
-    columns = held.shape[1]
-    return [
-        pltpu.make_async_copy(
-            weights.at[:, pl.ds(s, TILE)], held.at[:, pl.ds(s, TILE)], sems.at[n]
-        )
-        for n, s in enumerate(range(0, columns, TILE))
-    ]
-
-
-def first_kernel(weights, probes, out, held, sems):
-    copies = row_copies(weights, held, sems)
-    for copy in copies:
-        copy.start()
-    for n, copy in enumerate(copies):
-        copy.wait()
-        s = n * TILE
-        out[s : s + TILE, :] = mm(held[s : s + TILE, :], probes[...]).astype(BF16)
-
-
-def power_kernel(weights, sketch, out, held, turned, back, sems):
-    copies = column_copies(weights, held, sems)
-    for copy in copies:
-        copy.start()
+def first_kernel(weights, probes, out):
+    for s in range(0, out.shape[0], 2 * TILE):
+        out[s : s + 2 * TILE, :] = mm(weights[s : s + 2 * TILE, :], probes[...]).astype(BF16)
+
+
+def power_kernel(weights, sketch, out, turned, back):
     turned[...] = sketch[...].T
-    for n, copy in enumerate(copies):
-        copy.wait()
-        s = n * TILE
-        back[s : s + TILE, :] = mm(turned[...], held[:, s : s + TILE]).astype(BF16).T
-    for s in range(0, out.shape[0], TILE):
-        out[s : s + TILE, :] = (mm(held[s : s + TILE, :], back[...]) * (1.0 / D)).astype(BF16)
+    for s in range(0, weights.shape[1], TILE):
+        back[s : s + TILE, :] = mm(turned[...], weights[:, s : s + TILE]).astype(BF16).T
+    for s in range(0, out.shape[0], 2 * TILE):
+        rows = weights[s : s + 2 * TILE, :]
+        out[s : s + 2 * TILE, :] = (mm(rows, back[...]) * (1.0 / D)).astype(BF16)
 
 
 def pair_kernel(pairing, received, out):
@@ -161,11 +128,8 @@
 
 
 def final_kernel(
-    start, weights, sketch, basis, factors, held, turned, mixed, gram, inverse, work, sems
+    start, weights, sketch, basis, factors, turned, mixed, gram, inverse, work
 ):
-    copies = column_copies(weights, held, sems)
-    for copy in copies:
-        copy.start()
     turned[...] = sketch[...].T
     gram[...] = mm(turned[...], sketch[...])
     inverse_factor(gram, inverse, work)
@@ -177,10 +141,8 @@
     own_count = basis.shape[0]
     own = sketch[pl.ds(pl.multiple_of(start[0] * own_count, own_count), own_count), :]
     basis[...] = (mm(own, high.T) + mm(own, low.T)) * math.sqrt(FF)
-    for n, copy in enumerate(copies):
-        copy.wait()
-        s = n * TILE
-        factors[:, s : s + TILE] = mm(mixed[...], held[:, s : s + TILE]).astype(BF16)
+    for s in range(0, weights.shape[1], TILE):
+        factors[:, s : s + TILE] = mm(mixed[...], weights[:, s : s + TILE]).astype(BF16)
 
 
 def exchange(value):
@@ -194,9 +156,6 @@
     rank = probe_block.shape[1]
     device_count = lax.axis_size("ep") * lax.axis_size("tp")
     own_count = rows // lax.axis_size("tp")
-    held = pltpu.VMEM((rows, columns), BF16)
-    row_sems = pltpu.SemaphoreType.DMA((rows // TILE,))
-    column_sems = pltpu.SemaphoreType.DMA((columns // TILE,))
     sketch_shape = jax.ShapeDtypeStruct((rows, rank), BF16)
     chunks = (device_count, rows // device_count, rank)
 
@@ -207,6 +166,7 @@
             out_shape=jax.ShapeDtypeStruct(chunks, BF16),
             in_specs=[smem_spec(), vmem_spec()],
             out_specs=vmem_spec(),
+            compiler_params=params(),
             name="pair",
         )(pairing, received)
         return exchange(paired).reshape(rows, rank)
@@ -214,46 +174,42 @@
     partial_value = pl.pallas_call(
         first_kernel,
         out_shape=sketch_shape,
-        in_specs=[any_spec(), vmem_spec()],
+        in_specs=[vmem_spec(), vmem_spec()],
         out_specs=vmem_spec(),
-        scratch_shapes=[held, row_sems],
         compiler_params=params(),
         name="first",
     )(weight_block, probe_block)
+    start = lax.axis_index("tp").reshape(1).astype(jnp.int32)
+    partial_value, start = lax.optimization_barrier((partial_value, start))
     sketch = relay(partial_value)
     for _ in range(POWER):
         partial_value = pl.pallas_call(
             power_kernel,
             out_shape=sketch_shape,
-            in_specs=[any_spec(), vmem_spec()],
+            in_specs=[vmem_spec(), vmem_spec()],
             out_specs=vmem_spec(),
             scratch_shapes=[
-                held,
                 pltpu.VMEM((rank, rows), BF16),
                 pltpu.VMEM((columns, rank), BF16),
-                column_sems,
             ],
             compiler_params=params(),
             name="power",
         )(weight_block, sketch)
         sketch = relay(partial_value)
-    start = lax.axis_index("tp").reshape(1).astype(jnp.int32)
     basis, factors = pl.pallas_call(
         final_kernel,
         out_shape=(
             jax.ShapeDtypeStruct((own_count, rank), F32),
             jax.ShapeDtypeStruct((rank, columns), BF16),
         ),
-        in_specs=[smem_spec(), any_spec(), vmem_spec()],
+        in_specs=[smem_spec(), vmem_spec(), vmem_spec()],
         out_specs=(vmem_spec(), vmem_spec()),
         scratch_shapes=[
-            held,
             pltpu.VMEM((rank, rows), BF16),
             pltpu.VMEM((rank, rows), BF16),
             pltpu.VMEM((rank, rank), F32),
             pltpu.VMEM((rank, rank), F32),
             pltpu.VMEM((BLOCK, 2 * BLOCK), F32),
-            column_sems,
         ],
         compiler_params=params(),
         name="final",

time: 211 us -> 177 us (0.84)
  Pallas kernels: 47.6 us -> 26.1 us
  blocking collectives: 125 us -> 146 us
  waiting for transfers between devices: 19.5 us -> 0 us
  local copies, waits for them, and re-layouts: 13.5 us -> 4.26 us
  starting transfers between devices: 3.83 us -> 0 us
    all_to_all x5 -> x6, blocking collectives: 125 us -> 146 us  [exchange(): lax.all_to_all(value, ('ep', 'tp'), split_axis=0, concat_axis=0, tiled=True)]
    all_to_all x1 -> x0, waiting for transfers between devices: 19.5 us -> none  [exchange(): lax.all_to_all(value, ('ep', 'tp'), split_axis=0, concat_axis=0, tiled=True)]
    pallas_call x3, Pallas kernels: 22.8 us -> 10 us  [the longest x2 7.97 us: per_device(): pl.pallas_call(power_kernel, out_shape=sketch_shape, in_specs=[vmem_spec(...]
    unnamed x10 -> x8, local copies, waits for them, and re-layouts: 13.5 us -> 4.26 us
    pallas_call x3, Pallas kernels: 7.15 us -> 2.05 us  [relay(): pl.pallas_call(pair_kernel, out_shape=jax.ShapeDtypeStruct(chunks, BF16),...]
    all_to_all x1 -> x0, starting transfers between devices: 3.83 us -> none  [exchange(): lax.all_to_all(value, ('ep', 'tp'), split_axis=0, concat_axis=0, tiled=True)]
    pallas_call x1, Pallas kernels: 17.7 us -> 14 us  [per_device(): pl.pallas_call(final_kernel, out_shape=(jax.ShapeDtypeStruct((own_count,...]
  transfers between devices with their start and end apart: 1 -> 0, of which waited for: 1 -> 0; matrix products, arithmetic and copies ran while one was open for 0% -> 0% of each run, Pallas kernels for 0% -> 0%
where the time goes in v2:
time: 177 us
  blocking collectives  146 us (82%)
  Pallas kernels  26.1 us (15%)
  local copies, waits for them, and re-layouts  4.26 us (2%)
    all_to_all x6, blocking collectives, exchange(): lax.all_to_all(value, ('ep', 'tp'), split_axis=0, concat_axis=0, tiled=True)  146 us
    pallas_call x1, Pallas kernels, per_device(): pl.pallas_call(final_kernel, out_shape=(jax.ShapeDtypeStruct((own_count,...  14 us
    pallas_call x2, Pallas kernels, per_device(): pl.pallas_call(power_kernel, out_shape=sketch_shape, in_specs=[vmem_spec(...  7.97 us
    unnamed x8, local copies, waits for them, and re-layouts  4.26 us

profile of v2, /device:TPU:1, one launch (start us, length us, event | category | flops | bytes accessed | tf_op | source)
XLA Modules:
  0.0 177.0 jit_solution(5122273684460223512)
XLA Ops:
  0.6 0.0 copy-start.3
  0.6 0.0 copy-start
  0.7 3.1 %copy-done = bf16[1,2048,1792]{2,1,0:T(8,128)(2,1)S(1)} copy-done((bf16[1,2048,1792]{2,1,0:T(8,128)(2,1)S(1)}, bf16[1,2048,1792]{2,1,0:T(8,128)(2,1)}, u32[]{:S(2)}) %copy-start) | copy-done | bytes 7340056
  3.7 0.0 copy-start.2
  3.7 1.2 copy-done.2
  4.9 0.0 copy-start.1
  4.9 2.1 %first.1 = bf16[2048,256]{1,0:T(8,128)(2,1)S(1)} custom-call(bf16[2048,1792]{1,0:T(8,128)(2,1)S(1)} %bitcast.11, bf16[1792,256]{1,0:T(8,128)(2,1)S(1)} %bitcast.21), custom_call_target="tpu_custom_call" | custom-call | tf_op jit(solution)/shard_map/first/pallas_call | solution.py:174
  7.0 30.7 %all_to_all.30.received = bf16[128,16,256]{2,1,0:T(8,128)(2,1)S(1)} all-to-all(bf16[128,16,256]{2,1,0:T(8,128)(2,1)S(1)} %bitcast.20), channel_id=1, replica_groups=mesh['ep'=32,'tp'=4] {'ep','tp'}, dimensions={0} | all-to-all | bytes 2097152 | tf_op jit(solution)/shard_map/all_to_all | solution.py:149
  37.7 0.0 copy-done.3
  37.7 0.7 pair.3
  38.4 23.0 %all_to_all.31 = bf16[128,16,256]{2,1,0:T(8,128)(2,1)S(1)} all-to-all(bf16[128,16,256]{2,1,0:T(8,128)(2,1)S(1)} %pair.3), channel_id=1, replica_groups=mesh['ep'=32,'tp'=4] {'ep','tp'}, dimensions={0} | all-to-all | bytes 2097152 | tf_op jit(solution)/shard_map/all_to_all | solution.py:149
  61.4 0.0 copy-done.1
  61.4 4.0 %power.2 = bf16[2048,256]{1,0:T(8,128)(2,1)S(1)} custom-call(bf16[2048,1792]{1,0:T(8,128)(2,1)S(1)} %bitcast.12, bf16[2048,256]{1,0:T(8,128)(2,1)S(1)} %bitcast.16), custom_call_target="tpu_custom_call" | custom-call | tf_op jit(solution)/shard_map/power/pallas_call | solution.py:186
  65.4 23.0 %all_to_all.32.received = bf16[128,16,256]{2,1,0:T(8,128)(2,1)S(1)} all-to-all(bf16[128,16,256]{2,1,0:T(8,128)(2,1)S(1)} %bitcast.17), channel_id=1, replica_groups=mesh['ep'=32,'tp'=4] {'ep','tp'}, dimensions={0} | all-to-all | bytes 2097152 | tf_op jit(solution)/shard_map/all_to_all | solution.py:149
  88.5 0.7 pair.4
  89.2 23.0 %all_to_all.33 = bf16[128,16,256]{2,1,0:T(8,128)(2,1)S(1)} all-to-all(bf16[128,16,256]{2,1,0:T(8,128)(2,1)S(1)} %pair.4), channel_id=1, replica_groups=mesh['ep'=32,'tp'=4] {'ep','tp'}, dimensions={0} | all-to-all | bytes 2097152 | tf_op jit(solution)/shard_map/all_to_all | solution.py:149
  112.2 4.0 %power.3 = bf16[2048,256]{1,0:T(8,128)(2,1)S(1)} custom-call(bf16[2048,1792]{1,0:T(8,128)(2,1)S(1)} %bitcast.13, bf16[2048,256]{1,0:T(8,128)(2,1)S(1)} %bitcast.18), custom_call_target="tpu_custom_call" | custom-call | tf_op jit(solution)/shard_map/power/pallas_call | solution.py:186
  116.2 23.0 %all_to_all.34.received = bf16[128,16,256]{2,1,0:T(8,128)(2,1)S(1)} all-to-all(bf16[128,16,256]{2,1,0:T(8,128)(2,1)S(1)} %bitcast.19), channel_id=1, replica_groups=mesh['ep'=32,'tp'=4] {'ep','tp'}, dimensions={0} | all-to-all | bytes 2097152 | tf_op jit(solution)/shard_map/all_to_all | solution.py:149
  139.2 0.7 pair.5
  139.9 23.0 %all_to_all.35 = bf16[128,16,256]{2,1,0:T(8,128)(2,1)S(1)} all-to-all(bf16[128,16,256]{2,1,0:T(8,128)(2,1)S(1)} %pair.5), channel_id=1, replica_groups=mesh['ep'=32,'tp'=4] {'ep','tp'}, dimensions={0} | all-to-all | bytes 2097152 | tf_op jit(solution)/shard_map/all_to_all | solution.py:149
  163.0 14.0 %final.1 = (f32[512,256]{1,0:T(8,128)}, bf16[256,1792]{1,0:T(8,128)(2,1)}) custom-call(s32[1]{0:T(128)} %bitcast.2.start, bf16[2048,1792]{1,0:T(8,128)(2,1)S(1)} %bitcast.14, bf16[2048,256]{1,0:T(8,128)(2,1)S(1)} %bitcast.15), custom_call_target="tpu_custom_call" | custom-call | tf_op jit(solution)/shard_map/final/pallas_call | solution.py:199
Async XLA Ops:
  0.6 37.1 %copy-start.3 = (s32[32]{0:T(128)S(1)}, s32[32]{0:T(128)}, u32[]{:S(2)}) copy-start(s32[32]{0:T(128)} %pairing.5) | copy-start | bytes 388
  0.6 3.1 %copy-start = (bf16[1,2048,1792]{2,1,0:T(8,128)(2,1)S(1)}, bf16[1,2048,1792]{2,1,0:T(8,128)(2,1)}, u32[]{:S(2)}) copy-start(bf16[1,2048,1792]{2,1,0:T(8,128)(2,1)} %param.3) | copy-start | bytes 22020100
  3.7 1.2 copy-start.2
  4.9 56.5 %copy-start.1 = (bf16[1,2048,1792]{2,1,0:T(8,128)(2,1)S(1)}, bf16[1,2048,1792]{2,1,0:T(8,128)(2,1)}, u32[]{:S(2)}) copy-start(bf16[1,2048,1792]{2,1,0:T(8,128)(2,1)} %param.3) | copy-start | bytes 22020100

commit v3 on v2

--- a/solution.py
+++ b/solution.py
@@ -13,7 +13,7 @@
 F32 = jnp.float32
 BF16 = jnp.bfloat16
 HIGHEST = lax.Precision.HIGHEST
-BLOCK = 64
+BLOCK = 128
 TILE = 256
 VMEM_LIMIT = 24 * 1024 * 1024
 
@@ -24,6 +24,10 @@
 
 def vmem_spec():
     return pl.BlockSpec(memory_space=pltpu.VMEM)
+
+
+def any_spec():
+    return pl.BlockSpec(memory_space=pl.ANY)
 
 
 def smem_spec():
@@ -64,8 +68,27 @@
         out[pl.ds(b * tp_count, tp_count)] = spread
 
 
-def factor_block(work):
-    sublane = lax.broadcasted_iota(jnp.int32, (8, 2 * BLOCK), 0)
+def exact(a, b):
+    return jnp.dot(a, b, precision=HIGHEST, preferred_element_type=F32)
+
+
+def exact_turned(a, b):
+    turned = (((0,), (0,)), ((), ()))
+    return lax.dot_general(a, b, turned, precision=HIGHEST, preferred_element_type=F32)
+
+
+def identity(n):
+    rows = lax.broadcasted_iota(jnp.int32, (n, n), 0)
+    columns = lax.broadcasted_iota(jnp.int32, (n, n), 1)
+    return jnp.where(rows == columns, 1.0, 0.0).astype(F32)
+
+
+def factor_block(work, beside):
+    lanes = work.shape[0]
+    halves = range(work.shape[1] // lanes)
+    count = lanes // 8
+    sublane = lax.broadcasted_iota(jnp.int32, (8, lanes), 0)
+    ones = jnp.ones((8, lanes), F32)
 
     def row(x, i):
         return jnp.broadcast_to(x[i : i + 1, :], x.shape)
@@ -73,76 +96,124 @@
     def column(x, c):
         return jnp.broadcast_to(x[:, c : c + 1], x.shape)
 
-    count = BLOCK // 8
-    groups = [work[8 * g : 8 * g + 8, :] for g in range(count)]
-    for p in range(count):
-        columns = {
-            g: [column(groups[g], 8 * p + i) for i in range(8)] for g in range(p, count)
-        }
-        pivots = jnp.ones_like(groups[p])
-        for i in range(8):
-            pivot = row(columns[p][i], i)
-            pivots = jnp.where(sublane == i, pivot, pivots)
+    def place(g, h):
+        return slice(8 * g, 8 * g + 8), slice(lanes * h, lanes * h + lanes)
+
+    groups = [[work[place(g, h)] for h in halves] for g in range(count)]
+    for p in range(0, count, 2):
+        if beside:
+            beside.pop(0)()
+        base = 8 * p
+        reduced = [list(groups[p]), list(groups[p + 1])]
+        final = [list(groups[p]), list(groups[p + 1])]
+        columns = [[column(groups[p + q][0], base + i) for q in range(2)] for i in range(16)]
+        inverses = [ones, ones]
+        pivots = [ones, ones]
+        for i in range(16):
+            q, r = divmod(i, 8)
+            pivot = row(columns[i][q], r)
             inverse = 1.0 / pivot
-            across = [row(columns[p][c], i) for c in range(i + 1, 8)]
-            pivot_row = row(groups[p], i)
-            for g in range(p, count):
-                if g == p and i == 7:
-                    continue
-                scaled = columns[g][i] * inverse
-                if g == p:
-                    scaled = jnp.where(sublane > i, scaled, 0.0)
-                for n, c in enumerate(range(i + 1, 8)):
-                    columns[g][c] = columns[g][c] - scaled * across[n]
-                groups[g] = groups[g] - scaled * pivot_row
-        work[8 * p : 8 * p + 8, :] = groups[p] * lax.rsqrt(pivots)
-
-
-def inverse_factor(gram, inverse, work):
-    size = gram.shape[0]
-
-    def identity(n):
-        rows = lax.broadcasted_iota(jnp.int32, (n, n), 0)
-        columns = lax.broadcasted_iota(jnp.int32, (n, n), 1)
-        return jnp.where(rows == columns, 1.0, 0.0).astype(F32)
-
-    inverse[...] = identity(size)
-    for s in range(0, size, BLOCK):
-        e = s + BLOCK
-        work[:, 0:BLOCK] = gram[s:e, s:e]
-        work[:, BLOCK : 2 * BLOCK] = identity(BLOCK)
-        factor_block(work)
-        block = work[:, BLOCK : 2 * BLOCK]
-        done = jnp.dot(block, inverse[s:e, :], precision=HIGHEST, preferred_element_type=F32)
-        inverse[s:e, :] = done
-        if e < size:
-            upper = jnp.dot(block, gram[s:e, :], precision=HIGHEST, preferred_element_type=F32)
-            left = upper[:, e:]
-            turned = (((0,), (0,)), ((), ()))
-            gram[e:, :] = gram[e:, :] - lax.dot_general(
-                left, upper, turned, precision=HIGHEST, preferred_element_type=F32
-            )
-            inverse[e:, :] = inverse[e:, :] - lax.dot_general(
-                left, done, turned, precision=HIGHEST, preferred_element_type=F32
-            )
+            pivots[q] = jnp.where(sublane == r, pivot, pivots[q])
+            inverses[q] = jnp.where(sublane == r, inverse, inverses[q])
+            scaled = [columns[i][0] * inverse, columns[i][1] * inverse]
+            scaled[q] = jnp.where(sublane == r, 0.0, scaled[q])
+            for c in range(i + 1, 16):
+                across = row(columns[c][q], r)
+                columns[c] = [columns[c][k] - scaled[k] * across for k in range(2)]
+            for h in halves:
+                pivot_row = row(reduced[q][h], r)
+                final[q][h] = jnp.where(sublane == r, pivot_row, final[q][h])
+                for k in range(2):
+                    reduced[k][h] = reduced[k][h] - scaled[k] * pivot_row
+        for q in range(2):
+            scale = lax.rsqrt(pivots[q])
+            for h in halves:
+                work[place(p + q, h)] = final[q][h] * scale
+                reduced[q][h] = reduced[q][h] * inverses[q]
+        solved = [[row(reduced[c // 8][h], c % 8) for h in halves] for c in range(16)]
+        for g in range(p + 2, count):
+            left = [column(groups[g][0], base + c) for c in range(16)]
+            for h in halves:
+                terms = [left[c] * solved[c][h] for c in range(16)]
+                while len(terms) > 1:
+                    terms = [terms[k] + terms[k + 1] for k in range(0, len(terms), 2)]
+                groups[g][h] = groups[g][h] - terms[0]
+    while beside:
+        beside.pop(0)()
+
+
+def inverse_factor(gram, inverse, work, beside):
+    n = BLOCK
+    upper_left, lower_left = slice(0, n), slice(n, 2 * n)
+    work[:, :n] = gram[upper_left, :n]
+    work[:, n:] = identity(n)
+    share = (len(beside) + 1) // 2
+    factor_block(work, beside[:share])
+    top = work[:, n:]
+    cross = exact(top, gram[upper_left, n:])
+    work[:, :n] = gram[lower_left, n:] - exact_turned(cross, cross)
+    work[:, n:] = identity(n)
+
+    def fill():
+        inverse[upper_left, :n] = top
+        inverse[upper_left, n:] = jnp.zeros((n, n), F32)
+        inverse[lower_left, :n] = exact_turned(cross, top)
+
+    factor_block(work, [fill] + beside[share:])
+    bottom = work[:, n:]
+    inverse[lower_left, :n] = -exact(bottom, inverse[lower_left, :n])
+    inverse[lower_left, n:] = bottom
 
 
 def final_kernel(
-    start, weights, sketch, basis, factors, turned, mixed, gram, inverse, work
+    start,
+    weights,
+    sketch,
+    basis,
+    factors,
+    turned,
+    high_part,
+    low_part,
+    gram,
+    inverse,
+    work,
+    own_basis,
+    own_factors,
+    sems,
 ):
+    columns = weights.shape[1]
     turned[...] = sketch[...].T
     gram[...] = mm(turned[...], sketch[...])
-    inverse_factor(gram, inverse, work)
+
+    def project(s):
+        def run():
+            product = mm(turned[...], weights[:, s : s + TILE])
+            high = product.astype(BF16)
+            high_part[:, s : s + TILE] = high
+            low_part[:, s : s + TILE] = (product - high.astype(F32)).astype(BF16)
+
+        return run
+
+    inverse_factor(gram, inverse, work, [project(s) for s in range(0, columns, TILE)])
     high = inverse[...].astype(BF16)
     low = (inverse[...] - high.astype(F32)).astype(BF16)
-    for s in range(0, sketch.shape[0], TILE):
-        part = turned[:, s : s + TILE]
-        mixed[:, s : s + TILE] = (mm(high, part) + mm(low, part)).astype(BF16)
-    own_count = basis.shape[0]
+    copies = []
+    for n, s in enumerate(range(0, columns, TILE)):
+        part = high_part[:, s : s + TILE]
+        rest = mm(low, part) + mm(high, low_part[:, s : s + TILE])
+        own_factors[:, s : s + TILE] = (mm(high, part) + rest).astype(BF16)
+        place = pl.ds(s, TILE)
+        copies.append(
+            pltpu.make_async_copy(own_factors.at[:, place], factors.at[:, place], sems.at[n])
+        )
+        copies[-1].start()
+    own_count = own_basis.shape[0]
     own = sketch[pl.ds(pl.multiple_of(start[0] * own_count, own_count), own_count), :]
-    basis[...] = (mm(own, high.T) + mm(own, low.T)) * math.sqrt(FF)
-    for s in range(0, weights.shape[1], TILE):
-        factors[:, s : s + TILE] = mm(mixed[...], weights[:, s : s + TILE]).astype(BF16)
+    own_basis[...] = (mm(own, high.T) + mm(own, low.T)) * math.sqrt(FF)
+    copies.append(pltpu.make_async_copy(own_basis, basis, sems.at[len(copies)]))
+    copies[-1].start()
+    for copy in copies:
+        copy.wait()
 
 
 def exchange(value):
@@ -203,13 +274,17 @@
             jax.ShapeDtypeStruct((rank, columns), BF16),
         ),
         in_specs=[smem_spec(), vmem_spec(), vmem_spec()],
-        out_specs=(vmem_spec(), vmem_spec()),
+        out_specs=(any_spec(), any_spec()),
         scratch_shapes=[
             pltpu.VMEM((rank, rows), BF16),
-            pltpu.VMEM((rank, rows), BF16),
+            pltpu.VMEM((rank, columns), BF16),
+            pltpu.VMEM((rank, columns), BF16),
             pltpu.VMEM((rank, rank), F32),
             pltpu.VMEM((rank, rank), F32),
             pltpu.VMEM((BLOCK, 2 * BLOCK), F32),
+            pltpu.VMEM((own_count, rank), F32),
+            pltpu.VMEM((rank, columns), BF16),
+            pltpu.SemaphoreType.DMA((columns // TILE + 1,)),
         ],
         compiler_params=params(),
         name="final",

time: 177 us -> 174 us (0.983)
  Pallas kernels: 26.1 us -> 22.3 us
    pallas_call x1, Pallas kernels: 14 us -> 10.2 us  [per_device(): pl.pallas_call(final_kernel, out_shape=(jax.ShapeDtypeStruct((own_count,...]
where the time goes in v3:
time: 174 us; the launch traced here: 173 us
  blocking collectives  146 us (84%)
  Pallas kernels  22.3 us (13%)
  local copies, waits for them, and re-layouts  4.26 us (2%)
    all_to_all x6, blocking collectives, exchange(): lax.all_to_all(value, ('ep', 'tp'), split_axis=0, concat_axis=0, tiled=True)  146 us
    pallas_call x1, Pallas kernels, per_device(): pl.pallas_call(final_kernel, out_shape=(jax.ShapeDtypeStruct((own_count,...  10.2 us
    pallas_call x2, Pallas kernels, per_device(): pl.pallas_call(power_kernel, out_shape=sketch_shape, in_specs=[vmem_spec(...  7.97 us
    unnamed x8, local copies, waits for them, and re-layouts  4.26 us

profile of v3, /device:TPU:1, one launch (start us, length us, event | category | flops | bytes accessed | tf_op | source)
XLA Modules:
  0.0 173.4 jit_solution(8331309601404289746)
XLA Ops:
  0.6 0.0 copy-start.3
  0.6 0.0 copy-start
  0.7 3.1 %copy-done = bf16[1,2048,1792]{2,1,0:T(8,128)(2,1)S(1)} copy-done((bf16[1,2048,1792]{2,1,0:T(8,128)(2,1)S(1)}, bf16[1,2048,1792]{2,1,0:T(8,128)(2,1)}, u32[]{:S(2)}) %copy-start) | copy-done | bytes 7340056
  3.7 0.0 copy-start.2
  3.7 1.2 copy-done.2
  4.9 0.0 copy-start.1
  4.9 2.1 %first.1 = bf16[2048,256]{1,0:T(8,128)(2,1)S(1)} custom-call(bf16[2048,1792]{1,0:T(8,128)(2,1)S(1)} %bitcast.11, bf16[1792,256]{1,0:T(8,128)(2,1)S(1)} %bitcast.21), custom_call_target="tpu_custom_call" | custom-call | tf_op jit(solution)/shard_map/first/pallas_call | solution.py:245
  7.0 30.7 %all_to_all.30.received = bf16[128,16,256]{2,1,0:T(8,128)(2,1)S(1)} all-to-all(bf16[128,16,256]{2,1,0:T(8,128)(2,1)S(1)} %bitcast.20), channel_id=1, replica_groups=mesh['ep'=32,'tp'=4] {'ep','tp'}, dimensions={0} | all-to-all | bytes 2097152 | tf_op jit(solution)/shard_map/all_to_all | solution.py:220
  37.7 0.0 copy-done.3
  37.7 0.7 pair.3
  38.4 23.0 %all_to_all.31 = bf16[128,16,256]{2,1,0:T(8,128)(2,1)S(1)} all-to-all(bf16[128,16,256]{2,1,0:T(8,128)(2,1)S(1)} %pair.3), channel_id=1, replica_groups=mesh['ep'=32,'tp'=4] {'ep','tp'}, dimensions={0} | all-to-all | bytes 2097152 | tf_op jit(solution)/shard_map/all_to_all | solution.py:220
  61.4 0.0 copy-done.1
  61.4 4.0 %power.2 = bf16[2048,256]{1,0:T(8,128)(2,1)S(1)} custom-call(bf16[2048,1792]{1,0:T(8,128)(2,1)S(1)} %bitcast.12, bf16[2048,256]{1,0:T(8,128)(2,1)S(1)} %bitcast.16), custom_call_target="tpu_custom_call" | custom-call | tf_op jit(solution)/shard_map/power/pallas_call | solution.py:257
  65.4 23.0 %all_to_all.32.received = bf16[128,16,256]{2,1,0:T(8,128)(2,1)S(1)} all-to-all(bf16[128,16,256]{2,1,0:T(8,128)(2,1)S(1)} %bitcast.17), channel_id=1, replica_groups=mesh['ep'=32,'tp'=4] {'ep','tp'}, dimensions={0} | all-to-all | bytes 2097152 | tf_op jit(solution)/shard_map/all_to_all | solution.py:220
  88.5 0.7 pair.4
  89.2 23.0 %all_to_all.33 = bf16[128,16,256]{2,1,0:T(8,128)(2,1)S(1)} all-to-all(bf16[128,16,256]{2,1,0:T(8,128)(2,1)S(1)} %pair.4), channel_id=1, replica_groups=mesh['ep'=32,'tp'=4] {'ep','tp'}, dimensions={0} | all-to-all | bytes 2097152 | tf_op jit(solution)/shard_map/all_to_all | solution.py:220
  112.2 4.0 %power.3 = bf16[2048,256]{1,0:T(8,128)(2,1)S(1)} custom-call(bf16[2048,1792]{1,0:T(8,128)(2,1)S(1)} %bitcast.13, bf16[2048,256]{1,0:T(8,128)(2,1)S(1)} %bitcast.18), custom_call_target="tpu_custom_call" | custom-call | tf_op jit(solution)/shard_map/power/pallas_call | solution.py:257
  116.2 23.0 %all_to_all.34.received = bf16[128,16,256]{2,1,0:T(8,128)(2,1)S(1)} all-to-all(bf16[128,16,256]{2,1,0:T(8,128)(2,1)S(1)} %bitcast.19), channel_id=1, replica_groups=mesh['ep'=32,'tp'=4] {'ep','tp'}, dimensions={0} | all-to-all | bytes 2097152 | tf_op jit(solution)/shard_map/all_to_all | solution.py:220
  139.2 0.7 pair.5
  139.9 23.0 %all_to_all.35 = bf16[128,16,256]{2,1,0:T(8,128)(2,1)S(1)} all-to-all(bf16[128,16,256]{2,1,0:T(8,128)(2,1)S(1)} %pair.5), channel_id=1, replica_groups=mesh['ep'=32,'tp'=4] {'ep','tp'}, dimensions={0} | all-to-all | bytes 2097152 | tf_op jit(solution)/shard_map/all_to_all | solution.py:220
  163.0 10.2 %final.1 = (f32[512,256]{1,0:T(8,128)}, bf16[256,1792]{1,0:T(8,128)(2,1)}) custom-call(s32[1]{0:T(128)} %bitcast.2.start, bf16[2048,1792]{1,0:T(8,128)(2,1)S(1)} %bitcast.14, bf16[2048,256]{1,0:T(8,128)(2,1)S(1)} %bitcast.15), custom_call_target="tpu_custom_call" | custom-call | tf_op jit(solution)/shard_map/final/pallas_call | solution.py:270
Async XLA Ops:
  0.6 37.1 %copy-start.3 = (s32[32]{0:T(128)S(1)}, s32[32]{0:T(128)}, u32[]{:S(2)}) copy-start(s32[32]{0:T(128)} %pairing.5) | copy-start | bytes 388
  0.6 3.1 %copy-start = (bf16[1,2048,1792]{2,1,0:T(8,128)(2,1)S(1)}, bf16[1,2048,1792]{2,1,0:T(8,128)(2,1)}, u32[]{:S(2)}) copy-start(bf16[1,2048,1792]{2,1,0:T(8,128)(2,1)} %param.3) | copy-start | bytes 22020100
  3.7 1.2 copy-start.2
  4.9 56.5 %copy-start.1 = (bf16[1,2048,1792]{2,1,0:T(8,128)(2,1)S(1)}, bf16[1,2048,1792]{2,1,0:T(8,128)(2,1)}, u32[]{:S(2)}) copy-start(bf16[1,2048,1792]{2,1,0:T(8,128)(2,1)} %param.3) | copy-start | bytes 22020100

commit v4 on v3

--- a/solution.py
+++ b/solution.py
@@ -83,7 +83,7 @@
     return jnp.where(rows == columns, 1.0, 0.0).astype(F32)
 
 
-def factor_block(work, beside):
+def factor_block(work, solved_rows, beside):
     lanes = work.shape[0]
     halves = range(work.shape[1] // lanes)
     count = lanes // 8
@@ -99,14 +99,14 @@
     def place(g, h):
         return slice(8 * g, 8 * g + 8), slice(lanes * h, lanes * h + lanes)
 
-    groups = [[work[place(g, h)] for h in halves] for g in range(count)]
+    panel = [[work[place(g, h)] for h in halves] for g in range(2)]
     for p in range(0, count, 2):
         if beside:
             beside.pop(0)()
         base = 8 * p
-        reduced = [list(groups[p]), list(groups[p + 1])]
-        final = [list(groups[p]), list(groups[p + 1])]
-        columns = [[column(groups[p + q][0], base + i) for q in range(2)] for i in range(16)]
+        reduced = [list(panel[0]), list(panel[1])]
+        final = [list(panel[0]), list(panel[1])]
+        columns = [[column(panel[q][0], base + i) for q in range(2)] for i in range(16)]
         inverses = [ones, ones]
         pivots = [ones, ones]
         for i in range(16):
@@ -126,29 +126,41 @@
                 for k in range(2):
                     reduced[k][h] = reduced[k][h] - scaled[k] * pivot_row
         for q in range(2):
-            scale = lax.rsqrt(pivots[q])
             for h in halves:
-                work[place(p + q, h)] = final[q][h] * scale
                 reduced[q][h] = reduced[q][h] * inverses[q]
         solved = [[row(reduced[c // 8][h], c % 8) for h in halves] for c in range(16)]
-        for g in range(p + 2, count):
-            left = [column(groups[g][0], base + c) for c in range(16)]
+        panel = []
+        for g in range(p + 2, min(p + 4, count)):
+            below = [work[place(g, h)] for h in halves]
+            left = [column(below[0], base + c) for c in range(16)]
             for h in halves:
                 terms = [left[c] * solved[c][h] for c in range(16)]
                 while len(terms) > 1:
                     terms = [terms[k] + terms[k + 1] for k in range(0, len(terms), 2)]
-                groups[g][h] = groups[g][h] - terms[0]
+                below[h] = below[h] - terms[0]
+            panel.append(below)
+        rest = 8 * (p + 4)
+        if rest < lanes:
+            for q in range(2):
+                for h in halves:
+                    solved_rows[place(q, h)] = reduced[q][h]
+            update = exact(work[rest:, base : base + 16], solved_rows[...])
+            work[rest:, :] = work[rest:, :] - update
+        for q in range(2):
+            scale = lax.rsqrt(pivots[q])
+            for h in halves:
+                work[place(p + q, h)] = final[q][h] * scale
     while beside:
         beside.pop(0)()
 
 
-def inverse_factor(gram, inverse, work, beside):
+def inverse_factor(gram, inverse, work, solved_rows, beside):
     n = BLOCK
     upper_left, lower_left = slice(0, n), slice(n, 2 * n)
     work[:, :n] = gram[upper_left, :n]
     work[:, n:] = identity(n)
     share = (len(beside) + 1) // 2
-    factor_block(work, beside[:share])
+    factor_block(work, solved_rows, beside[:share])
     top = work[:, n:]
     cross = exact(top, gram[upper_left, n:])
     work[:, :n] = gram[lower_left, n:] - exact_turned(cross, cross)
@@ -159,7 +171,7 @@
         inverse[upper_left, n:] = jnp.zeros((n, n), F32)
         inverse[lower_left, :n] = exact_turned(cross, top)
 
-    factor_block(work, [fill] + beside[share:])
+    factor_block(work, solved_rows, [fill] + beside[share:])
     bottom = work[:, n:]
     inverse[lower_left, :n] = -exact(bottom, inverse[lower_left, :n])
     inverse[lower_left, n:] = bottom
@@ -177,6 +189,7 @@
     gram,
     inverse,
     work,
+    solved_rows,
     own_basis,
     own_factors,
     sems,
@@ -194,7 +207,8 @@
 
         return run
 
-    inverse_factor(gram, inverse, work, [project(s) for s in range(0, columns, TILE)])
+    pieces = [project(s) for s in range(0, columns, TILE)]
+    inverse_factor(gram, inverse, work, solved_rows, pieces)
     high = inverse[...].astype(BF16)
     low = (inverse[...] - high.astype(F32)).astype(BF16)
     copies = []
@@ -282,6 +296,7 @@
             pltpu.VMEM((rank, rank), F32),
             pltpu.VMEM((rank, rank), F32),
             pltpu.VMEM((BLOCK, 2 * BLOCK), F32),
+            pltpu.VMEM((16, 2 * BLOCK), F32),
             pltpu.VMEM((own_count, rank), F32),
             pltpu.VMEM((rank, columns), BF16),
             pltpu.SemaphoreType.DMA((columns // TILE + 1,)),

time: 174 us -> 172 us (0.989)
  no operation moved by 1% of the time
where the time goes in v4:
time: 172 us
  blocking collectives  146 us (85%)
  Pallas kernels  21.1 us (12%)
  local copies, waits for them, and re-layouts  4.26 us (2%)
    all_to_all x6, blocking collectives, exchange(): lax.all_to_all(value, ('ep', 'tp'), split_axis=0, concat_axis=0, tiled=True)  146 us
    pallas_call x1, Pallas kernels, per_device(): pl.pallas_call(final_kernel, out_shape=(jax.ShapeDtypeStruct((own_count,...  9 us
    pallas_call x2, Pallas kernels, per_device(): pl.pallas_call(power_kernel, out_shape=sketch_shape, in_specs=[vmem_spec(...  7.97 us
    unnamed x8, local copies, waits for them, and re-layouts  4.26 us

profile of v4, /device:TPU:1, one launch (start us, length us, event | category | flops | bytes accessed | tf_op | source)
XLA Modules:
  0.0 172.1 jit_solution(9773815943723981578)
XLA Ops:
  0.6 0.0 copy-start.3
  0.6 0.0 copy-start
  0.7 3.1 %copy-done = bf16[1,2048,1792]{2,1,0:T(8,128)(2,1)S(1)} copy-done((bf16[1,2048,1792]{2,1,0:T(8,128)(2,1)S(1)}, bf16[1,2048,1792]{2,1,0:T(8,128)(2,1)}, u32[]{:S(2)}) %copy-start) | copy-done | bytes 7340056
  3.7 0.0 copy-start.2
  3.7 1.2 copy-done.2
  4.9 0.0 copy-start.1
  4.9 2.1 %first.1 = bf16[2048,256]{1,0:T(8,128)(2,1)S(1)} custom-call(bf16[2048,1792]{1,0:T(8,128)(2,1)S(1)} %bitcast.11, bf16[1792,256]{1,0:T(8,128)(2,1)S(1)} %bitcast.21), custom_call_target="tpu_custom_call" | custom-call | tf_op jit(solution)/shard_map/first/pallas_call | solution.py:259
  7.0 30.7 %all_to_all.30.received = bf16[128,16,256]{2,1,0:T(8,128)(2,1)S(1)} all-to-all(bf16[128,16,256]{2,1,0:T(8,128)(2,1)S(1)} %bitcast.20), channel_id=1, replica_groups=mesh['ep'=32,'tp'=4] {'ep','tp'}, dimensions={0} | all-to-all | bytes 2097152 | tf_op jit(solution)/shard_map/all_to_all | solution.py:234
  37.7 0.0 copy-done.3
  37.7 0.7 pair.3
  38.4 23.0 %all_to_all.31 = bf16[128,16,256]{2,1,0:T(8,128)(2,1)S(1)} all-to-all(bf16[128,16,256]{2,1,0:T(8,128)(2,1)S(1)} %pair.3), channel_id=1, replica_groups=mesh['ep'=32,'tp'=4] {'ep','tp'}, dimensions={0} | all-to-all | bytes 2097152 | tf_op jit(solution)/shard_map/all_to_all | solution.py:234
  61.4 0.0 copy-done.1
  61.4 4.0 %power.2 = bf16[2048,256]{1,0:T(8,128)(2,1)S(1)} custom-call(bf16[2048,1792]{1,0:T(8,128)(2,1)S(1)} %bitcast.12, bf16[2048,256]{1,0:T(8,128)(2,1)S(1)} %bitcast.16), custom_call_target="tpu_custom_call" | custom-call | tf_op jit(solution)/shard_map/power/pallas_call | solution.py:271
  65.4 23.0 %all_to_all.32.received = bf16[128,16,256]{2,1,0:T(8,128)(2,1)S(1)} all-to-all(bf16[128,16,256]{2,1,0:T(8,128)(2,1)S(1)} %bitcast.17), channel_id=1, replica_groups=mesh['ep'=32,'tp'=4] {'ep','tp'}, dimensions={0} | all-to-all | bytes 2097152 | tf_op jit(solution)/shard_map/all_to_all | solution.py:234
  88.5 0.7 pair.4
  89.2 23.0 %all_to_all.33 = bf16[128,16,256]{2,1,0:T(8,128)(2,1)S(1)} all-to-all(bf16[128,16,256]{2,1,0:T(8,128)(2,1)S(1)} %pair.4), channel_id=1, replica_groups=mesh['ep'=32,'tp'=4] {'ep','tp'}, dimensions={0} | all-to-all | bytes 2097152 | tf_op jit(solution)/shard_map/all_to_all | solution.py:234
  112.2 4.0 %power.3 = bf16[2048,256]{1,0:T(8,128)(2,1)S(1)} custom-call(bf16[2048,1792]{1,0:T(8,128)(2,1)S(1)} %bitcast.13, bf16[2048,256]{1,0:T(8,128)(2,1)S(1)} %bitcast.18), custom_call_target="tpu_custom_call" | custom-call | tf_op jit(solution)/shard_map/power/pallas_call | solution.py:271
  116.2 23.0 %all_to_all.34.received = bf16[128,16,256]{2,1,0:T(8,128)(2,1)S(1)} all-to-all(bf16[128,16,256]{2,1,0:T(8,128)(2,1)S(1)} %bitcast.19), channel_id=1, replica_groups=mesh['ep'=32,'tp'=4] {'ep','tp'}, dimensions={0} | all-to-all | bytes 2097152 | tf_op jit(solution)/shard_map/all_to_all | solution.py:234
  139.2 0.7 pair.5
  139.9 23.0 %all_to_all.35 = bf16[128,16,256]{2,1,0:T(8,128)(2,1)S(1)} all-to-all(bf16[128,16,256]{2,1,0:T(8,128)(2,1)S(1)} %pair.5), channel_id=1, replica_groups=mesh['ep'=32,'tp'=4] {'ep','tp'}, dimensions={0} | all-to-all | bytes 2097152 | tf_op jit(solution)/shard_map/all_to_all | solution.py:234
  163.0 9.0 %final.1 = (f32[512,256]{1,0:T(8,128)}, bf16[256,1792]{1,0:T(8,128)(2,1)}) custom-call(s32[1]{0:T(128)} %bitcast.2.start, bf16[2048,1792]{1,0:T(8,128)(2,1)S(1)} %bitcast.14, bf16[2048,256]{1,0:T(8,128)(2,1)S(1)} %bitcast.15), custom_call_target="tpu_custom_call" | custom-call | tf_op jit(solution)/shard_map/final/pallas_call | solution.py:284
Async XLA Ops:
  0.6 37.1 %copy-start.3 = (s32[32]{0:T(128)S(1)}, s32[32]{0:T(128)}, u32[]{:S(2)}) copy-start(s32[32]{0:T(128)} %pairing.5) | copy-start | bytes 388
  0.6 3.1 %copy-start = (bf16[1,2048,1792]{2,1,0:T(8,128)(2,1)S(1)}, bf16[1,2048,1792]{2,1,0:T(8,128)(2,1)}, u32[]{:S(2)}) copy-start(bf16[1,2048,1792]{2,1,0:T(8,128)(2,1)} %param.3) | copy-start | bytes 22020100
  3.7 1.2 copy-start.2
  4.9 56.5 %copy-start.1 = (bf16[1,2048,1792]{2,1,0:T(8,128)(2,1)S(1)}, bf16[1,2048,1792]{2,1,0:T(8,128)(2,1)}, u32[]{:S(2)}) copy-start(bf16[1,2048,1792]{2,1,0:T(8,128)(2,1)} %param.3) | copy-start | bytes 22020100

commit v5 on v4

--- a/solution.py
+++ b/solution.py
@@ -43,9 +43,19 @@
         out[s : s + 2 * TILE, :] = mm(weights[s : s + 2 * TILE, :], probes[...]).astype(BF16)
 
 
+def turn_and_multiply(sketch, turned, other):
+    total = None
+    for s in range(0, sketch.shape[0], 2 * TILE):
+        part = sketch[s : s + 2 * TILE, :].T
+        turned[:, s : s + 2 * TILE] = part
+        product = mm(part, other[s : s + 2 * TILE, :TILE])
+        total = product if total is None else total + product
+    return total
+
+
 def power_kernel(weights, sketch, out, turned, back):
-    turned[...] = sketch[...].T
-    for s in range(0, weights.shape[1], TILE):
+    back[:TILE, :] = turn_and_multiply(sketch, turned, weights).astype(BF16).T
+    for s in range(TILE, weights.shape[1], TILE):
         back[s : s + TILE, :] = mm(turned[...], weights[:, s : s + TILE]).astype(BF16).T
     for s in range(0, out.shape[0], 2 * TILE):
         rows = weights[s : s + 2 * TILE, :]
@@ -157,24 +167,18 @@
 def inverse_factor(gram, inverse, work, solved_rows, beside):
     n = BLOCK
     upper_left, lower_left = slice(0, n), slice(n, 2 * n)
-    work[:, :n] = gram[upper_left, :n]
-    work[:, n:] = identity(n)
     share = (len(beside) + 1) // 2
+    work[:, : 2 * n] = gram[upper_left, :]
+    work[:, 2 * n :] = identity(n)
     factor_block(work, solved_rows, beside[:share])
-    top = work[:, n:]
-    cross = exact(top, gram[upper_left, n:])
-    work[:, :n] = gram[lower_left, n:] - exact_turned(cross, cross)
-    work[:, n:] = identity(n)
-
-    def fill():
-        inverse[upper_left, :n] = top
-        inverse[upper_left, n:] = jnp.zeros((n, n), F32)
-        inverse[lower_left, :n] = exact_turned(cross, top)
-
-    factor_block(work, solved_rows, [fill] + beside[share:])
-    bottom = work[:, n:]
-    inverse[lower_left, :n] = -exact(bottom, inverse[lower_left, :n])
-    inverse[lower_left, n:] = bottom
+    inverse[upper_left, :n] = work[:, 2 * n :]
+    inverse[upper_left, n:] = jnp.zeros((n, n), F32)
+    update = exact_turned(work[:, n : 2 * n], work[:, n:])
+    work[:, :n] = gram[lower_left, n:] - update[:, :n]
+    work[:, n : 2 * n] = -update[:, n:]
+    work[:, 2 * n :] = identity(n)
+    factor_block(work, solved_rows, beside[share:])
+    inverse[lower_left, :] = work[:, n:]
 
 
 def final_kernel(
@@ -195,8 +199,7 @@
     sems,
 ):
     columns = weights.shape[1]
-    turned[...] = sketch[...].T
-    gram[...] = mm(turned[...], sketch[...])
+    gram[...] = turn_and_multiply(sketch, turned, sketch)
 
     def project(s):
         def run():
@@ -295,8 +298,8 @@
             pltpu.VMEM((rank, columns), BF16),
             pltpu.VMEM((rank, rank), F32),
             pltpu.VMEM((rank, rank), F32),
-            pltpu.VMEM((BLOCK, 2 * BLOCK), F32),
-            pltpu.VMEM((16, 2 * BLOCK), F32),
+            pltpu.VMEM((BLOCK, 3 * BLOCK), F32),
+            pltpu.VMEM((16, 3 * BLOCK), F32),
             pltpu.VMEM((own_count, rank), F32),
             pltpu.VMEM((rank, columns), BF16),
             pltpu.SemaphoreType.DMA((columns // TILE + 1,)),

time: 172 us -> 172 us (level)
  no operation moved by 1% of the time
where the time goes in v5:
time: 172 us
  blocking collectives  146 us (85%)
  Pallas kernels  20.9 us (12%)
  local copies, waits for them, and re-layouts  4.26 us (2%)
    all_to_all x6, blocking collectives, exchange(): lax.all_to_all(value, ('ep', 'tp'), split_axis=0, concat_axis=0, tiled=True)  146 us
    pallas_call x1, Pallas kernels, per_device(): pl.pallas_call(final_kernel, out_shape=(jax.ShapeDtypeStruct((own_count,...  8.81 us
    pallas_call x2, Pallas kernels, per_device(): pl.pallas_call(power_kernel, out_shape=sketch_shape, in_specs=[vmem_spec(...  8 us
    unnamed x8, local copies, waits for them, and re-layouts  4.26 us

profile of v5, /device:TPU:1, one launch (start us, length us, event | category | flops | bytes accessed | tf_op | source)
XLA Modules:
  0.0 172.0 jit_solution(5595899747385779031)
XLA Ops:
  0.6 0.0 copy-start.3
  0.6 0.0 copy-start
  0.7 3.1 %copy-done = bf16[1,2048,1792]{2,1,0:T(8,128)(2,1)S(1)} copy-done((bf16[1,2048,1792]{2,1,0:T(8,128)(2,1)S(1)}, bf16[1,2048,1792]{2,1,0:T(8,128)(2,1)}, u32[]{:S(2)}) %copy-start) | copy-done | bytes 7340056
  3.7 0.0 copy-start.2
  3.7 1.2 copy-done.2
  4.9 0.0 copy-start.1
  4.9 2.1 %first.1 = bf16[2048,256]{1,0:T(8,128)(2,1)S(1)} custom-call(bf16[2048,1792]{1,0:T(8,128)(2,1)S(1)} %bitcast.11, bf16[1792,256]{1,0:T(8,128)(2,1)S(1)} %bitcast.21), custom_call_target="tpu_custom_call" | custom-call | tf_op jit(solution)/shard_map/first/pallas_call | solution.py:262
  7.0 30.7 %all_to_all.30.received = bf16[128,16,256]{2,1,0:T(8,128)(2,1)S(1)} all-to-all(bf16[128,16,256]{2,1,0:T(8,128)(2,1)S(1)} %bitcast.20), channel_id=1, replica_groups=mesh['ep'=32,'tp'=4] {'ep','tp'}, dimensions={0} | all-to-all | bytes 2097152 | tf_op jit(solution)/shard_map/all_to_all | solution.py:237
  37.7 0.0 copy-done.3
  37.7 0.7 pair.3
  38.4 23.0 %all_to_all.31 = bf16[128,16,256]{2,1,0:T(8,128)(2,1)S(1)} all-to-all(bf16[128,16,256]{2,1,0:T(8,128)(2,1)S(1)} %pair.3), channel_id=1, replica_groups=mesh['ep'=32,'tp'=4] {'ep','tp'}, dimensions={0} | all-to-all | bytes 2097152 | tf_op jit(solution)/shard_map/all_to_all | solution.py:237
  61.4 0.0 copy-done.1
  61.4 4.0 %power.2 = bf16[2048,256]{1,0:T(8,128)(2,1)S(1)} custom-call(bf16[2048,1792]{1,0:T(8,128)(2,1)S(1)} %bitcast.12, bf16[2048,256]{1,0:T(8,128)(2,1)S(1)} %bitcast.16), custom_call_target="tpu_custom_call" | custom-call | tf_op jit(solution)/shard_map/power/pallas_call | solution.py:274
  65.4 23.0 %all_to_all.32.received = bf16[128,16,256]{2,1,0:T(8,128)(2,1)S(1)} all-to-all(bf16[128,16,256]{2,1,0:T(8,128)(2,1)S(1)} %bitcast.17), channel_id=1, replica_groups=mesh['ep'=32,'tp'=4] {'ep','tp'}, dimensions={0} | all-to-all | bytes 2097152 | tf_op jit(solution)/shard_map/all_to_all | solution.py:237
  88.5 0.7 pair.4
  89.2 23.0 %all_to_all.33 = bf16[128,16,256]{2,1,0:T(8,128)(2,1)S(1)} all-to-all(bf16[128,16,256]{2,1,0:T(8,128)(2,1)S(1)} %pair.4), channel_id=1, replica_groups=mesh['ep'=32,'tp'=4] {'ep','tp'}, dimensions={0} | all-to-all | bytes 2097152 | tf_op jit(solution)/shard_map/all_to_all | solution.py:237
  112.2 4.0 %power.3 = bf16[2048,256]{1,0:T(8,128)(2,1)S(1)} custom-call(bf16[2048,1792]{1,0:T(8,128)(2,1)S(1)} %bitcast.13, bf16[2048,256]{1,0:T(8,128)(2,1)S(1)} %bitcast.18), custom_call_target="tpu_custom_call" | custom-call | tf_op jit(solution)/shard_map/power/pallas_call | solution.py:274
  116.2 23.0 %all_to_all.34.received = bf16[128,16,256]{2,1,0:T(8,128)(2,1)S(1)} all-to-all(bf16[128,16,256]{2,1,0:T(8,128)(2,1)S(1)} %bitcast.19), channel_id=1, replica_groups=mesh['ep'=32,'tp'=4] {'ep','tp'}, dimensions={0} | all-to-all | bytes 2097152 | tf_op jit(solution)/shard_map/all_to_all | solution.py:237
  139.3 0.7 pair.5
  139.9 23.0 %all_to_all.35 = bf16[128,16,256]{2,1,0:T(8,128)(2,1)S(1)} all-to-all(bf16[128,16,256]{2,1,0:T(8,128)(2,1)S(1)} %pair.5), channel_id=1, replica_groups=mesh['ep'=32,'tp'=4] {'ep','tp'}, dimensions={0} | all-to-all | bytes 2097152 | tf_op jit(solution)/shard_map/all_to_all | solution.py:237
  163.0 8.8 %final.1 = (f32[512,256]{1,0:T(8,128)}, bf16[256,1792]{1,0:T(8,128)(2,1)}) custom-call(s32[1]{0:T(128)} %bitcast.2.start, bf16[2048,1792]{1,0:T(8,128)(2,1)S(1)} %bitcast.14, bf16[2048,256]{1,0:T(8,128)(2,1)S(1)} %bitcast.15), custom_call_target="tpu_custom_call" | custom-call | tf_op jit(solution)/shard_map/final/pallas_call | solution.py:287
Async XLA Ops:
  0.6 37.1 %copy-start.3 = (s32[32]{0:T(128)S(1)}, s32[32]{0:T(128)}, u32[]{:S(2)}) copy-start(s32[32]{0:T(128)} %pairing.5) | copy-start | bytes 388
  0.6 3.1 %copy-start = (bf16[1,2048,1792]{2,1,0:T(8,128)(2,1)S(1)}, bf16[1,2048,1792]{2,1,0:T(8,128)(2,1)}, u32[]{:S(2)}) copy-start(bf16[1,2048,1792]{2,1,0:T(8,128)(2,1)} %param.3) | copy-start | bytes 22020100
  3.7 1.2 copy-start.2
  4.9 56.5 %copy-start.1 = (bf16[1,2048,1792]{2,1,0:T(8,128)(2,1)S(1)}, bf16[1,2048,1792]{2,1,0:T(8,128)(2,1)}, u32[]{:S(2)}) copy-start(bf16[1,2048,1792]{2,1,0:T(8,128)(2,1)} %param.3) | copy-start | bytes 22020100

commit v6 on v4

--- a/solution.py
+++ b/solution.py
@@ -212,20 +212,20 @@
     high = inverse[...].astype(BF16)
     low = (inverse[...] - high.astype(F32)).astype(BF16)
     copies = []
+    own_count = own_basis.shape[0]
+    own = sketch[pl.ds(pl.multiple_of(start[0] * own_count, own_count), own_count), :]
+    own_basis[...] = (mm(own, high.T) + mm(own, low.T)) * math.sqrt(FF)
+    copies.append(pltpu.make_async_copy(own_basis, basis, sems.at[len(copies)]))
+    copies[-1].start()
     for n, s in enumerate(range(0, columns, TILE)):
         part = high_part[:, s : s + TILE]
         rest = mm(low, part) + mm(high, low_part[:, s : s + TILE])
         own_factors[:, s : s + TILE] = (mm(high, part) + rest).astype(BF16)
         place = pl.ds(s, TILE)
         copies.append(
-            pltpu.make_async_copy(own_factors.at[:, place], factors.at[:, place], sems.at[n])
+            pltpu.make_async_copy(own_factors.at[:, place], factors.at[:, place], sems.at[n + 1])
         )
         copies[-1].start()
-    own_count = own_basis.shape[0]
-    own = sketch[pl.ds(pl.multiple_of(start[0] * own_count, own_count), own_count), :]
-    own_basis[...] = (mm(own, high.T) + mm(own, low.T)) * math.sqrt(FF)
-    copies.append(pltpu.make_async_copy(own_basis, basis, sems.at[len(copies)]))
-    copies[-1].start()
     for copy in copies:
         copy.wait()
 

time: 172 us -> 172 us (level)
  no operation moved by 1% of the time
where the time goes in v6:
time: 172 us
  blocking collectives  146 us (85%)
  Pallas kernels  20.9 us (12%)
  local copies, waits for them, and re-layouts  4.26 us (2%)
    all_to_all x6, blocking collectives, exchange(): lax.all_to_all(value, ('ep', 'tp'), split_axis=0, concat_axis=0, tiled=True)  146 us
    pallas_call x1, Pallas kernels, per_device(): pl.pallas_call(final_kernel, out_shape=(jax.ShapeDtypeStruct((own_count,...  8.85 us
    pallas_call x2, Pallas kernels, per_device(): pl.pallas_call(power_kernel, out_shape=sketch_shape, in_specs=[vmem_spec(...  7.97 us
    unnamed x8, local copies, waits for them, and re-layouts  4.26 us

profile of v6, /device:TPU:1, one launch (start us, length us, event | category | flops | bytes accessed | tf_op | source)
XLA Modules:
  0.0 172.0 jit_solution(2263775590001832639)
XLA Ops:
  0.6 0.0 copy-start.3
  0.6 0.0 copy-start
  0.7 3.1 %copy-done = bf16[1,2048,1792]{2,1,0:T(8,128)(2,1)S(1)} copy-done((bf16[1,2048,1792]{2,1,0:T(8,128)(2,1)S(1)}, bf16[1,2048,1792]{2,1,0:T(8,128)(2,1)}, u32[]{:S(2)}) %copy-start) | copy-done | bytes 7340056
  3.7 0.0 copy-start.2
  3.7 1.2 copy-done.2
  4.9 0.0 copy-start.1
  4.9 2.1 %first.1 = bf16[2048,256]{1,0:T(8,128)(2,1)S(1)} custom-call(bf16[2048,1792]{1,0:T(8,128)(2,1)S(1)} %bitcast.11, bf16[1792,256]{1,0:T(8,128)(2,1)S(1)} %bitcast.21), custom_call_target="tpu_custom_call" | custom-call | tf_op jit(solution)/shard_map/first/pallas_call | solution.py:259
  7.0 30.7 %all_to_all.30.received = bf16[128,16,256]{2,1,0:T(8,128)(2,1)S(1)} all-to-all(bf16[128,16,256]{2,1,0:T(8,128)(2,1)S(1)} %bitcast.20), channel_id=1, replica_groups=mesh['ep'=32,'tp'=4] {'ep','tp'}, dimensions={0} | all-to-all | bytes 2097152 | tf_op jit(solution)/shard_map/all_to_all | solution.py:234
  37.7 0.0 copy-done.3
  37.7 0.7 pair.3
  38.4 23.0 %all_to_all.31 = bf16[128,16,256]{2,1,0:T(8,128)(2,1)S(1)} all-to-all(bf16[128,16,256]{2,1,0:T(8,128)(2,1)S(1)} %pair.3), channel_id=1, replica_groups=mesh['ep'=32,'tp'=4] {'ep','tp'}, dimensions={0} | all-to-all | bytes 2097152 | tf_op jit(solution)/shard_map/all_to_all | solution.py:234
  61.4 0.0 copy-done.1
  61.4 4.0 %power.2 = bf16[2048,256]{1,0:T(8,128)(2,1)S(1)} custom-call(bf16[2048,1792]{1,0:T(8,128)(2,1)S(1)} %bitcast.12, bf16[2048,256]{1,0:T(8,128)(2,1)S(1)} %bitcast.16), custom_call_target="tpu_custom_call" | custom-call | tf_op jit(solution)/shard_map/power/pallas_call | solution.py:271
  65.4 23.0 %all_to_all.32.received = bf16[128,16,256]{2,1,0:T(8,128)(2,1)S(1)} all-to-all(bf16[128,16,256]{2,1,0:T(8,128)(2,1)S(1)} %bitcast.17), channel_id=1, replica_groups=mesh['ep'=32,'tp'=4] {'ep','tp'}, dimensions={0} | all-to-all | bytes 2097152 | tf_op jit(solution)/shard_map/all_to_all | solution.py:234
  88.5 0.7 pair.4
  89.2 23.0 %all_to_all.33 = bf16[128,16,256]{2,1,0:T(8,128)(2,1)S(1)} all-to-all(bf16[128,16,256]{2,1,0:T(8,128)(2,1)S(1)} %pair.4), channel_id=1, replica_groups=mesh['ep'=32,'tp'=4] {'ep','tp'}, dimensions={0} | all-to-all | bytes 2097152 | tf_op jit(solution)/shard_map/all_to_all | solution.py:234
  112.2 4.0 %power.3 = bf16[2048,256]{1,0:T(8,128)(2,1)S(1)} custom-call(bf16[2048,1792]{1,0:T(8,128)(2,1)S(1)} %bitcast.13, bf16[2048,256]{1,0:T(8,128)(2,1)S(1)} %bitcast.18), custom_call_target="tpu_custom_call" | custom-call | tf_op jit(solution)/shard_map/power/pallas_call | solution.py:271
  116.2 23.0 %all_to_all.34.received = bf16[128,16,256]{2,1,0:T(8,128)(2,1)S(1)} all-to-all(bf16[128,16,256]{2,1,0:T(8,128)(2,1)S(1)} %bitcast.19), channel_id=1, replica_groups=mesh['ep'=32,'tp'=4] {'ep','tp'}, dimensions={0} | all-to-all | bytes 2097152 | tf_op jit(solution)/shard_map/all_to_all | solution.py:234
  139.2 0.7 pair.5
  139.9 23.0 %all_to_all.35 = bf16[128,16,256]{2,1,0:T(8,128)(2,1)S(1)} all-to-all(bf16[128,16,256]{2,1,0:T(8,128)(2,1)S(1)} %pair.5), channel_id=1, replica_groups=mesh['ep'=32,'tp'=4] {'ep','tp'}, dimensions={0} | all-to-all | bytes 2097152 | tf_op jit(solution)/shard_map/all_to_all | solution.py:234
  163.0 8.9 %final.1 = (f32[512,256]{1,0:T(8,128)}, bf16[256,1792]{1,0:T(8,128)(2,1)}) custom-call(s32[1]{0:T(128)} %bitcast.2.start, bf16[2048,1792]{1,0:T(8,128)(2,1)S(1)} %bitcast.14, bf16[2048,256]{1,0:T(8,128)(2,1)S(1)} %bitcast.15), custom_call_target="tpu_custom_call" | custom-call | tf_op jit(solution)/shard_map/final/pallas_call | solution.py:284
Async XLA Ops:
  0.6 37.1 %copy-start.3 = (s32[32]{0:T(128)S(1)}, s32[32]{0:T(128)}, u32[]{:S(2)}) copy-start(s32[32]{0:T(128)} %pairing.5) | copy-start | bytes 388
  0.6 3.1 %copy-start = (bf16[1,2048,1792]{2,1,0:T(8,128)(2,1)S(1)}, bf16[1,2048,1792]{2,1,0:T(8,128)(2,1)}, u32[]{:S(2)}) copy-start(bf16[1,2048,1792]{2,1,0:T(8,128)(2,1)} %param.3) | copy-start | bytes 22020100
  3.7 1.2 copy-start.2
  4.9 56.5 %copy-start.1 = (bf16[1,2048,1792]{2,1,0:T(8,128)(2,1)S(1)}, bf16[1,2048,1792]{2,1,0:T(8,128)(2,1)}, u32[]{:S(2)}) copy-start(bf16[1,2048,1792]{2,1,0:T(8,128)(2,1)} %param.3) | copy-start | bytes 22020100
